TPU v7x, 256 devices: a whole 4x4x8 slice. The times are simulated.
256 devices in a mesh: gx: 4 (over x), gy: 8 (over y, core), gz: 8 (over z).
Axes of the slice: x: 4, y: 4, z: 8, core: 2. Of those that a mesh axis runs over, the one named last changes fastest.
Arguments:
- earlier_basis: float32 [8, 4, 16, 128, 1024], P(None, None, 'gx', 'gy', 'gz'), may hold values from -40 to 40
- diffusivity: float32 [4, 16, 128, 1024], P(None, 'gx', 'gy', 'gz'), may hold values from 0.5 to 4
- reaction: float32 [4, 4, 16, 128, 1024], P(None, None, 'gx', 'gy', 'gz'), may hold values from -4 to 4
Outputs:
- new_basis: float32 [4, 4, 16, 128, 1024], P(None, None, 'gx', 'gy', 'gz')
- coefficients: float32 [8, 4], replicated
- triangle: float32 [4, 4], replicated
All inputs are finite; a program needn't handle non-finite values.
Results may differ from a plain program's by a relative error of at most 0.00027.
Values sent between devices are 32-bit elements; how exact they have to be, the bound alone decides.
No kernel may reach another device: no remote copies, remote signals or barrier semaphores. Data moves between devices by JAX's collectives and lax.ppermute only.
A program may use at most 64 MiB of HBM per device.

v0:
```python
import functools

import jax
import jax.numpy as jnp
from jax import lax
from jax.experimental import pallas as pl
from jax.experimental.pallas import tpu as pltpu
from jax.sharding import PartitionSpec as P

SPECIES = 4
STEPS = 4
EARLIER = 8
SHIFTS = (6.0, 9.0, 14.0, 17.0)
DAMPING = 0.2
AXES = ("gx", "gy", "gz")

VECTORS = EARLIER + STEPS
SLOT = {}
for _b in range(VECTORS):
    for _a in range(_b + 1):
        SLOT[(_a, _b)] = len(SLOT)

WIDE = 2
DEEP = 4
ROWS = 24
V_PLANES = tuple(range(-WIDE, 4 + WIDE))
R_PLANES = tuple(range(-1, 5))
V_BASE = 0
D_BASE = SPECIES * len(V_PLANES)
R_BASE = 2 * D_BASE
PLANES = R_BASE + SPECIES * SPECIES * len(R_PLANES)
HALVES = SPECIES // 2
SIDES = 2 * HALVES + HALVES * SPECIES
BLOCKS = SIDES // 2


def v_at(s, x):
    return V_BASE + s * len(V_PLANES) + x + WIDE


def d_at(s, x):
    return D_BASE + s * len(V_PLANES) + x + WIDE


def r_at(s, t, x):
    return R_BASE + (s * SPECIES + t) * len(R_PLANES) + x + 1


def iota(shape, dim):
    return lax.broadcasted_iota(jnp.int32, shape, dim)


def roll(value, shift, axis):
    shift %= value.shape[axis]
    return pltpu.roll(value, shift, axis) if shift else value


def x_faces(q_ref, d_ref, r_ref, low_ref, high_ref, v_out, d_out, sems):
    copies = []
    for face, planes, plane in ((low_ref, pl.ds(0, WIDE), 0), (high_ref, pl.ds(4 - WIDE, WIDE), 3)):
        for n, source in enumerate((q_ref.at[EARLIER - 1, :, planes], d_ref.at[:, planes])):
            target = face.at[pl.ds(n * SPECIES * WIDE, SPECIES * WIDE)]
            copies.append((source, target.reshape((SPECIES, WIDE) + face.shape[1:])))
        target = face.at[pl.ds(2 * SPECIES * WIDE, SPECIES * SPECIES)]
        copies.append((r_ref.at[:, :, plane], target.reshape((SPECIES, SPECIES) + face.shape[1:])))
    copies += [(q_ref.at[EARLIER - 1], v_out), (d_ref, d_out)]
    started = [pltpu.make_async_copy(a, b, sems.at[n]) for n, (a, b) in enumerate(copies)]
    for copy in started:
        copy.start()
    for copy in started:
        copy.wait()


def own_planes(v_ref, d_ref, r_ref, before_ref, after_ref):
    def pick(own, slot, width, x):
        if x < 0:
            return lambda rows: before_ref[slot + x + width, rows]
        if x > 3:
            return lambda rows: after_ref[slot + x - 4, rows]
        return lambda rows: own(x, rows)

    planes = []
    for s in range(SPECIES):
        for x in V_PLANES:
            planes.append(pick(lambda x, rows, s=s: v_ref[s, x, rows], s * WIDE, WIDE, x))
    for s in range(SPECIES):
        for x in V_PLANES:
            planes.append(pick(lambda x, rows, s=s: d_ref[s, x, rows], (SPECIES + s) * WIDE, WIDE, x))
    for s in range(SPECIES):
        for t in range(SPECIES):
            slot = 2 * SPECIES * WIDE + s * SPECIES + t
            for x in R_PLANES:
                planes.append(pick(lambda x, rows, s=s, t=t: r_ref[s, t, x, rows], slot, 1, x))
    return planes


def y_places():
    places, used = {}, [0, 0]

    def put(message, planes, rows):
        per = 8 // rows
        for n, plane in enumerate(planes):
            places[plane] = (message, used[message] + n // per, n % per, rows)
        used[message] += len(planes) // per

    near, far, own = [], [], []
    for base in (v_at, d_at):
        for s in range(SPECIES):
            for x in V_PLANES:
                (own if 0 <= x < 4 else near if -1 <= x < 5 else far).append(base(s, x))
    for s in range(SPECIES):
        for t in range(SPECIES):
            for x in R_PLANES:
                (own if 0 <= x < 4 else far).append(r_at(s, t, x))
    put(0, own, DEEP)
    put(1, near, DEEP)
    put(1, far, 2)
    return places, used


Y_PLACES, Y_TILES = y_places()


def y_faces(message, planes, low_ref, high_ref):
    row = iota((8, 128), 0)
    low, high = [None] * Y_TILES[message], [None] * Y_TILES[message]
    for plane, (number, tile, place, rows) in Y_PLACES.items():
        if number != message:
            continue
        first = roll(planes[plane](pl.ds(0, 8)), rows * place, 0)
        final = roll(planes[plane](pl.ds(8, 8)), rows * place + rows, 0)
        here = row // rows == place
        low[tile] = first if low[tile] is None else jnp.where(here, first, low[tile])
        high[tile] = final if high[tile] is None else jnp.where(here, final, high[tile])
    for tile in range(Y_TILES[message]):
        low_ref[tile] = low[tile]
        high_ref[tile] = high[tile]


def own_faces(v_ref, d_ref, r_ref, y_low, y_high, z_low, z_high):
    planes = own_planes(v_ref, d_ref, r_ref, None, None)
    y_faces(0, planes, y_low, y_high)
    for block, found in enumerate(z_groups(True)):
        z_low[block], z_high[block] = pack_z(found, lambda plane: planes[plane](pl.ds(0, 16)), 16)


def more_y_faces(before_ref, after_ref, low_ref, high_ref):
    y_faces(1, own_planes(None, None, None, before_ref, after_ref), low_ref, high_ref)


def side_planes(side):
    found = []
    for half in range(2):
        for x in V_PLANES:
            if side < 2 * HALVES:
                s = side % HALVES * 2 + half
                found.append(v_at(s, x) if side < HALVES else d_at(s, x))
            else:
                pair, t = divmod(side - 2 * HALVES, SPECIES)
                found.append(r_at(2 * pair + half, t, x) if x in R_PLANES else None)
    return found


def z_groups(own):
    blocks = [[] for _ in range(SIDES // 4)]
    for side in range(SIDES):
        for slot, plane in enumerate(side_planes(side)):
            if plane is not None and own == (WIDE <= slot % 8 < WIDE + 4):
                group = (2 * slot + 8 * (side % 4 // 2) + side % 2) % 32
                blocks[side // 4].append((plane, group))
    return blocks


def z_edge_groups():
    blocks = [[] for _ in range(BLOCKS)]
    for side in range(SIDES):
        for slot, plane in enumerate(side_planes(side)):
            if plane is not None:
                blocks[side // 2].append((plane, 2 * slot + side % 2))
    return blocks


def pack_z(planes, value_of, rows):
    group = iota((rows, 128), 1) // DEEP
    low = high = jnp.zeros((rows, 128), jnp.float32)
    for plane, k in planes:
        value = value_of(plane)
        low = jnp.where(group == k, roll(value, DEEP * k, 1), low)
        high = jnp.where(group == k, roll(value, DEEP * k + DEEP, 1), high)
    return low, high


def more_z_faces(x_before, x_after, own_before, own_after, more_before, more_after, edge_ref, low_ref, high_ref):
    planes = own_planes(None, None, None, x_before, x_after)
    top = iota((8, 128), 0) < DEEP
    befores, afters = (own_before, more_before), (own_after, more_after)
    for block, found in enumerate(z_groups(False)):
        low, high = pack_z(found, lambda plane: planes[plane](pl.ds(0, 16)), 16)
        for half in range(2):
            low_ref[2 * block + half] = low[8 * half : 8 * half + 8]
            high_ref[2 * block + half] = high[8 * half : 8 * half + 8]

    def value_of(plane):
        message, tile, place, rows = Y_PLACES[plane]
        after = roll(afters[message][tile], -rows * place, 0)
        before = roll(befores[message][tile], 8 - rows - rows * place, 0)
        edge_ref[plane] = jnp.where(top, after, before)
        return edge_ref[plane]

    for block, found in enumerate(z_edge_groups()):
        low_ref[BLOCKS + block], high_ref[BLOCKS + block] = pack_z(found, value_of, 8)


def unpack_z(side, own_before, own_after, more_before, more_after):
    lane = iota((16, 128), 1)
    block, turned, part = side // 4, side % 4 // 2, side % 2
    own = (lane // 8 % 8 >= WIDE) & (lane // 8 % 8 < WIDE + 4)
    if turned:
        own = ~own

    def rows(own_ref, more_ref):
        more = jnp.concatenate([more_ref[2 * block], more_ref[2 * block + 1]], 0)
        return jnp.where(own, own_ref[block], more)

    def join(before, after, shift):
        early = iota(before.shape, 1) % 8 < DEEP
        return jnp.where(early, roll(before, -shift - DEEP * part, 1), roll(after, DEEP - shift - DEEP * part, 1))

    main = join(rows(own_before, more_before), rows(own_after, more_after), 32 * turned)
    edge = join(more_before[BLOCKS + side // 2], more_after[BLOCKS + side // 2], 0)
    return jnp.concatenate([main, edge], 0)


class Planes:
    def __init__(self, planes, edge_ref):
        self.planes, self.edge_ref = planes, edge_ref

    def __getitem__(self, plane):
        return jnp.concatenate([self.planes[plane](pl.ds(0, 16)), self.edge_ref[plane]], 0)


def masks():
    first = {axis: lax.axis_index(axis) == 0 for axis in AXES}
    final = {axis: lax.axis_index(axis) == lax.axis_size(axis) - 1 for axis in AXES}

    def keep(flag):
        return jnp.where(flag, 0.0, 1.0).astype(jnp.float32)

    row, lane = iota((ROWS, 128), 0), iota((ROWS, 128), 1)
    main = jnp.where(row < 16, 1.0, jnp.where(row < 16 + DEEP, keep(final["gy"]), keep(first["gy"])))
    slot = lane // 8 % 8
    side = main * jnp.where(lane % 8 < DEEP, keep(first["gz"]), keep(final["gz"]))
    before, after = keep(first["gx"]), keep(final["gx"])
    side = side * jnp.where(slot < WIDE, before, jnp.where(slot < WIDE + 4, 1.0, after))
    return main, side, before, after


def mask_of(x, main, before, after):
    if 0 <= x < 4:
        return main
    return main * (before if x < 0 else after)


def next_y(value):
    return roll(value, -1, 0)


def slot_of(s, x):
    return 64 * (s % 2) + 8 * (x + WIDE)


def columns(planes, value_of):
    group = iota((ROWS, 128), 1) // 8
    found = []
    for half in range(HALVES):
        value = jnp.zeros((ROWS, 128), jnp.float32)
        for s in (2 * half, 2 * half + 1):
            for x in planes:
                place = slot_of(s, x)
                value = jnp.where(group == place // 8, roll(value_of(s, x), place + DEEP, 1), value)
        found.append(value)
    return found


def next_z(value, side, place):
    lane = iota((ROWS, 128), 1)
    return jnp.where(lane == 127, roll(side, 127 - place - DEEP, 1), roll(value, -1, 1))


def previous_z(value, side, place):
    lane = iota((ROWS, 128), 1)
    return jnp.where(lane == 0, roll(side, -(place + DEEP - 1), 1), roll(value, 1, 1))


def side_next_z(side, edge):
    return roll(jnp.where(iota((ROWS, 128), 1) % 8 == DEEP, edge, side), -1, 1)


def side_previous_z(side, edge):
    return roll(jnp.where(iota((ROWS, 128), 1) % 8 == DEEP - 1, edge, side), 1, 1)


def cx_at(s, x):
    return s * 7 + x + 2


def cy_at(s, x):
    return SPECIES * 7 + s * 6 + x + 1


def cz_at(s, x):
    return SPECIES * 13 + s * 6 + x + 1


def back_at(s, x):
    return SPECIES * 19 + s * 6 + x + 1


CONDUCTS = SPECIES * 25


def conduct(d_of, d_side, c_ref, c_side):
    for s in range(SPECIES):
        for x in V_PLANES:
            d = d_of(s, x)
            if x < V_PLANES[-1]:
                c_ref[cx_at(s, x)] = 0.5 * (d + d_of(s, x + 1))
            if x in R_PLANES:
                c_ref[cy_at(s, x)] = 0.5 * (d + next_y(d))
                c_ref[cz_at(s, x)] = 0.5 * (d + next_z(d, d_side[s // 2], slot_of(s, x)))
                c_ref[back_at(s, x)] = 0.5 * (d + previous_z(d, d_side[s // 2], slot_of(s, x)))
    edges = columns(R_PLANES, d_of)
    for half in range(HALVES):
        d = d_side[half]
        c_side[4 * half] = 0.5 * (d + roll(d, -8, 1))
        c_side[4 * half + 1] = 0.5 * (d + next_y(d))
        c_side[4 * half + 2] = 0.5 * (d + side_next_z(d, edges[half]))
        c_side[4 * half + 3] = 0.5 * (d + side_previous_z(d, edges[half]))


def step(degree, planes, v_of, v_side, main_ref, side_ref, c_ref, c_side, mask, store, sides=True):
    lane = iota((ROWS, 128), 1)
    for x in planes:
        factor = DAMPING * mask_of(x, mask[0], *mask[2:])
        here = [v_of(t, x) for t in range(SPECIES)]
        for s in range(SPECIES):
            half, place, v = s // 2, slot_of(s, x), here[s]
            value = v * (1.0 - SHIFTS[degree])
            value = value + c_ref[cz_at(s, x)] * (v - next_z(v, v_side[half], place))
            value = value + c_ref[back_at(s, x)] * (v - previous_z(v, v_side[half], place))
            for t in range(SPECIES):
                value = value + main_ref[r_at(s, t, x)] * here[t]
            value = value + c_ref[cx_at(s, x)] * (v - v_of(s, x + 1))
            value = value + c_ref[cx_at(s, x - 1)] * (v - v_of(s, x - 1))
            along = c_ref[cy_at(s, x)] * (v - next_y(v))
            value = value + (along - roll(along, 1, 0))
            store(s, x, value * factor)
    if not sides:
        return None
    edges = columns(planes, v_of)
    both = []
    for half in range(HALVES):
        other = roll(v_side[half], 64, 1)
        both.append(jnp.where(lane < 64, v_side[half], other))
        both.append(jnp.where(lane < 64, other, v_side[half]))
    result = []
    for half in range(HALVES):
        v = v_side[half]
        value = v * (1.0 - SHIFTS[degree])
        value = value + c_side[4 * half + 2] * (v - side_next_z(v, edges[half]))
        value = value + c_side[4 * half + 3] * (v - side_previous_z(v, edges[half]))
        for t in range(SPECIES):
            value = value + side_ref[2 * HALVES + SPECIES * half + t] * both[t]
        across = c_side[4 * half] * (v - roll(v, -8, 1))
        value = value + (across - roll(across, 8, 1))
        along = c_side[4 * half + 1] * (v - next_y(v))
        value = value + (along - roll(along, 1, 0))
        result.append(value * (DAMPING * mask[1]))
    return result


def put_own(out_ref, s, x, value):
    out_ref[8 * s + 2 * x] = value[:8]
    out_ref[8 * s + 2 * x + 1] = value[8:16]


def first_steps(v_ref, d_ref, r_ref, x_before, x_after, edge_ref, own_before, own_after, more_before, more_after, v1_ref, v2_ref, wide_ref, wide_side, low_ref, high_ref, side_ref, c_ref, c_side, v_in, v_mid):
    main_ref = Planes(own_planes(v_ref, d_ref, r_ref, x_before, x_after), edge_ref)
    lane = iota((ROWS, 128), 1)
    for side in range(SIDES):
        side_ref[side] = unpack_z(side, own_before, own_after, more_before, more_after)
    mask = masks()

    def inside(plane, x):
        return main_ref[plane] * mask_of(x, mask[0], *mask[2:])

    v_side = [side_ref[half] * mask[1] for half in range(HALVES)]
    d_side = [side_ref[HALVES + half] * mask[1] for half in range(HALVES)]
    for s in range(SPECIES):
        for x in V_PLANES:
            v_mid[v_at(s, x)] = inside(d_at(s, x), x)
            v_in[v_at(s, x)] = inside(v_at(s, x), x)
    conduct(lambda s, x: v_mid[v_at(s, x)], d_side, c_ref, c_side)

    def store_mid(s, x, value):
        v_mid[v_at(s, x)] = value
        if 0 <= x < 4:
            put_own(v1_ref, s, x, value)

    def store_wide(s, x, value):
        wide_ref[4 * s + x] = value
        put_own(v2_ref, s, x, value)

    more = (main_ref, side_ref, c_ref, c_side, mask)
    v_side = step(0, R_PLANES, lambda s, x: v_in[v_at(s, x)], v_side, *more, store_mid)
    v_side = step(1, range(4), lambda s, x: v_mid[v_at(s, x)], v_side, *more, store_wide)
    for half in range(HALVES):
        wide_side[half] = v_side[half]
    slot = lane // 8 % 8
    for face, start, shift in ((low_ref, 0, -16), (high_ref, 4 - WIDE, 16)):
        for s in range(SPECIES):
            for n in range(WIDE):
                face[s * WIDE + n] = wide_ref[4 * s + start + n]
        kept = (slot >= start + WIDE) & (slot < start + 2 * WIDE)
        face[SPECIES * WIDE] = jnp.where(kept, v_side[0], roll(v_side[1], shift, 1))


def last_steps(r_ref, x_before, x_after, edge_ref, side_ref, c_ref, c_side, wide_ref, wide_side, before_ref, after_ref, q_ref, v1_ref, v2_ref, sums_in, v3_ref, v4_ref, sums_ref, v_in, v_mid):
    main_ref = Planes(own_planes(None, None, r_ref, x_before, x_after), edge_ref)
    mask = masks()
    for s in range(SPECIES):
        for face, start, factor in ((before_ref, -WIDE, mask[2]), (after_ref, 4, mask[3])):
            for n in range(WIDE):
                v_in[v_at(s, start + n)] = face[s * WIDE + n] * factor
    slot = iota((ROWS, 128), 1) // 8 % 8
    before, after = before_ref[SPECIES * WIDE] * mask[2], after_ref[SPECIES * WIDE] * mask[3]
    v_side = []
    for half in range(HALVES):
        value = jnp.where(slot < WIDE, roll(before, -32 - 16 * half, 1), wide_side[half])
        v_side.append(jnp.where(slot >= WIDE + 4, roll(after, 32 + 16 * half, 1), value))

    def first(s, x):
        return wide_ref[4 * s + x] if 0 <= x < 4 else v_in[v_at(s, x)]

    def store_mid(s, x, value):
        v_mid[v_at(s, x)] = value
        if 0 <= x < 4:
            put_own(v3_ref, s, x, value)

    def store_last(s, x, value):
        put_own(v4_ref, s, x, value)

    more = (main_ref, side_ref, c_ref, c_side, mask)
    v_side = step(2, R_PLANES, first, v_side, *more, store_mid)
    step(3, range(4), lambda s, x: v_mid[v_at(s, x)], v_side, *more, store_last, sides=False)

    def load(i):
        return [q_ref[a, i] for a in range(EARLIER)] + [v1_ref[i], v2_ref[i], v3_ref[i], v4_ref[i]]

    row = sums_in[...] + products(new_pairs(2) + new_pairs(3), load, q_ref.shape[1])
    sums_ref[...] = jnp.broadcast_to(jnp.sum(row, 0, keepdims=True), sums_ref.shape)


def middle_products(q_ref, v1_ref, v2_ref, before_ref, out_ref):
    def load(i):
        return [q_ref[a, i] for a in range(EARLIER)] + [v1_ref[i], v2_ref[i]]

    out_ref[...] = before_ref[...] + products(new_pairs(0) + new_pairs(1), load, q_ref.shape[1])


def products(pairs, load, count):
    def body(i, sums):
        values = load(i)
        return tuple(total + values[a] * values[b] for total, (a, b) in zip(sums, pairs))

    zero = jnp.zeros((8, 128), jnp.float32)
    sums = lax.fori_loop(0, count, body, (zero,) * len(pairs))
    lane = lax.broadcasted_iota(jnp.int32, (8, 128), 1)
    row = zero
    for total, pair in zip(sums, pairs):
        row = jnp.where(lane == SLOT[pair], jnp.sum(total, 1, keepdims=True), row)
    return row


def earlier_products(q_ref, out_ref):
    pairs = [(a, b) for b in range(EARLIER) for a in range(b + 1)]
    out_ref[...] = products(pairs, lambda i: [q_ref[a, i] for a in range(EARLIER)], q_ref.shape[1])


def new_pairs(number):
    return [(a, EARLIER + number) for a in range(EARLIER + number + 1)]


def finish_kernel(entries, sums_ref, q_ref, *refs):
    v_refs, (new_ref, coeff_ref, triangle_ref) = refs[:STEPS], refs[STEPS:]
    total = sums_ref[0]
    for i in range(1, sums_ref.shape[0]):
        total = total + sums_ref[i]
    total = jnp.broadcast_to(jnp.sum(total, 0, keepdims=True), total.shape) * (1.0 / entries)

    def entry(a, b):
        k = SLOT[(min(a, b), max(a, b))]
        return jnp.broadcast_to(total[:, k : k + 1], total.shape)

    coeff = [[entry(i, EARLIER + j) for j in range(STEPS)] for i in range(EARLIER)]
    overlap = {(a, b): entry(a, b) for b in range(EARLIER) for a in range(b + 1)}
    gram = {}
    for k in range(STEPS):
        mixed = []
        for i in range(EARLIER):
            term = -2.0 * coeff[i][k]
            for m in range(EARLIER):
                term = term + overlap[(min(i, m), max(i, m))] * coeff[m][k]
            mixed.append(term)
        for j in range(k, STEPS):
            value = entry(EARLIER + k, EARLIER + j)
            for i in range(EARLIER):
                value = value + coeff[i][j] * mixed[i]
            gram[(j, k)] = value
    factor, inverse = {}, []
    for k in range(STEPS):
        pivot = gram[(k, k)]
        for m in range(k):
            pivot = pivot - factor[(k, m)] * factor[(k, m)]
        factor[(k, k)] = jnp.sqrt(pivot)
        inverse.append(1.0 / factor[(k, k)])
        for j in range(k + 1, STEPS):
            value = gram[(j, k)]
            for m in range(k):
                value = value - factor[(j, m)] * factor[(k, m)]
            factor[(j, k)] = value * inverse[k]
    row = lax.broadcasted_iota(jnp.int32, total.shape, 0)
    lane = lax.broadcasted_iota(jnp.int32, total.shape, 1)
    table = jnp.zeros_like(total)
    for i in range(EARLIER):
        for j in range(STEPS):
            table = jnp.where((row == j) & (lane == i), coeff[i][j], table)
    coeff_ref[...] = table[:STEPS, :EARLIER]
    table = jnp.zeros_like(total)
    for (j, k), value in factor.items():
        table = jnp.where((row == k) & (lane == j), value, table)
    triangle_ref[...] = table[:STEPS, :STEPS]

    def body(n, carry):
        earlier = [q_ref[i, n] for i in range(EARLIER)]
        done = []
        for j in range(STEPS):
            value = v_refs[j][n]
            for i in range(EARLIER):
                value = value - coeff[i][j] * earlier[i]
            for k in range(j):
                value = value - factor[(j, k)] * done[k]
            done.append(value * inverse[j])
            new_ref[j, n] = done[j]
        return carry

    lax.fori_loop(0, q_ref.shape[1], body, 0)


def call(body, outs, cost, *args, **more):
    return pl.pallas_call(
        body,
        out_shape=[jax.ShapeDtypeStruct(shape, jnp.float32) for shape in outs],
        cost_estimate=pl.CostEstimate(flops=cost, bytes_accessed=cost, transcendentals=0),
        compiler_params=pltpu.CompilerParams(vmem_limit_bytes=24 << 20),
        **more,
    )(*args)


def shifts(axis):
    count = lax.axis_size(axis)
    up = [(i, (i + 1) % count) for i in range(count)]
    return up, [(target, source) for source, target in up]


def exchange(axis, low, high):
    up, down = shifts(axis)
    return lax.ppermute(high, axis, up), lax.ppermute(low, axis, down)


def on_device(earlier_basis, diffusivity, reaction):
    span_x, span_y, span_z = diffusivity.shape[1:]
    tiles = SPECIES * span_x * span_y // 8
    devices = 1
    for axis in AXES:
        devices *= lax.axis_size(axis)
    entries = tiles * 8 * span_z * devices
    in_hbm = pl.BlockSpec(memory_space=pltpu.HBM)
    given = (earlier_basis, diffusivity, reaction)
    face = (2 * SPECIES * WIDE + SPECIES * SPECIES, span_y, span_z)
    field = diffusivity.shape
    low, high, *kept = call(
        x_faces,
        [face, face, field, field],
        1 << 20,
        *[pltpu.with_memory_space_constraint(a, pltpu.HBM) for a in given],
        in_specs=[in_hbm] * 3,
        scratch_shapes=[pltpu.SemaphoreType.DMA((8,))],
    )
    x_halos = exchange("gx", low, high)
    kept.append(reaction)
    face = (Y_TILES[0], 8, span_z)
    z_face = (SIDES // 4, 16, span_z)
    own = call(own_faces, [face, face, z_face, z_face], 1 << 20, *kept)
    y_own = exchange("gy", *own[:2])
    up, down = shifts("gz")
    z_before = lax.ppermute(own[3], "gz", up)
    z_after = lax.ppermute(own[2], "gz", down)
    z_own = (z_before, z_after)
    face = (Y_TILES[1], 8, span_z)
    faces = call(more_y_faces, [face, face], 1 << 20, *x_halos)
    y_more = exchange("gy", *faces)
    face = (2 * BLOCKS, 8, span_z)
    edge, low, high = call(more_z_faces, [(PLANES, 8, span_z), face, face], 1 << 20, *x_halos, *y_own, *y_more)
    z_more = exchange("gz", low, high)
    basis = earlier_basis.reshape(EARLIER, tiles, 8, span_z)
    (sums,) = call(earlier_products, [(8, span_z)], 4 << 20, basis)
    own = (tiles, 8, span_z)
    scratch = [pltpu.VMEM((D_BASE, ROWS, span_z), jnp.float32)] * 2
    several = [
        (count, ROWS, span_z)
        for count in (SPECIES * span_x, HALVES, SPECIES * WIDE + 1, SPECIES * WIDE + 1, SIDES, CONDUCTS, 4 * HALVES)
    ]
    v1, v2, wide, wide_side, low, high, side, conducts, side_conducts = call(
        first_steps,
        [own, own] + several,
        1 << 20,
        *kept,
        *x_halos,
        edge,
        *z_own,
        *z_more,
        scratch_shapes=scratch,
    )
    halos = exchange("gx", low, high)
    (sums,) = call(middle_products, [(8, span_z)], 4 << 20, basis, v1, v2, sums)
    v3, v4, rows = call(
        last_steps,
        [own, own, (devices, span_z)],
        1 << 20,
        reaction,
        *x_halos,
        edge,
        side,
        conducts,
        side_conducts,
        wide,
        wide_side,
        *halos,
        basis,
        v1,
        v2,
        sums,
        scratch_shapes=scratch,
    )
    rows = lax.all_to_all(rows.reshape(devices, 1, span_z), AXES, 0, 0)
    new, coeff, triangle = call(
        functools.partial(finish_kernel, entries),
        [(STEPS, tiles, 8, span_z), (STEPS, EARLIER), (STEPS, STEPS)],
        1 << 20,
        rows.reshape(devices // 8, 8, span_z),
        basis,
        v1,
        v2,
        v3,
        v4,
    )
    return new.reshape((STEPS, SPECIES, span_x, span_y, span_z)), coeff.T, triangle


def solution(mesh):
    in_specs = (
        P(None, None, "gx", "gy", "gz"),
        P(None, "gx", "gy", "gz"),
        P(None, None, "gx", "gy", "gz"),
    )
    out_specs = (P(None, None, "gx", "gy", "gz"), P(), P())
    return jax.shard_map(
        on_device, mesh=mesh, in_specs=in_specs, out_specs=out_specs, check_vma=False
    )
```

profile of v0, /device:TPU:1, one launch (start us, length us, event | category | flops | bytes accessed | tf_op | source)
XLA Modules:
  0.0 64.8 jit_solution(87156745222770233)
XLA Ops:
  0.6 1.3 %shard_map.58 = (f32[32,16,128]{2,1,0:T(8,128)S(1)}, f32[32,16,128]{2,1,0:T(8,128)S(1)}, f32[4,4,16,128]{3,2,1,0:T(8,128)S(1)}, f32[4,4,16,128]{3,2,1,0:T(8,128)S(1)}) custom-call(f32[8,4,4,16,128]{4,3,2,1,0:T(8,128)} %q_ref.1, f32[4,4,16,128]{3,2,1,0:T(8,128)} %d_ref.1, f32[4,4,4,16,128]{4,3,2,1,0:T(8,128)} %r_ref.7), custom_call_target="tpu_custom_call" | custom-call | flops 1048576 | bytes 1048576 | tf_op jit(solution)/shard_map/pallas_call | solution.py:561
  2.0 2.1 %collective-permute-start = (f32[32,16,128]{2,1,0:T(8,128)S(1)}, f32[32,16,128]{2,1,0:T(8,128)S(1)}, u32[]{:S(2)}, u32[]{:S(2)}) collective-permute-start(f32[32,16,128]{2,1,0:T(8,128)S(1)} %get-tuple-element.31), channel_id=1, source_target_pairs={{0,64},{64,128},{128,192},{192,0},{1,65},{65,129},{129,193},{193,1... | collective-permute-start | bytes 786440 | tf_op jit(solution)/shard_map/ppermute | solution.py:578
  4.1 1.4 %collective-permute-start.1 = (f32[32,16,128]{2,1,0:T(8,128)S(1)}, f32[32,16,128]{2,1,0:T(8,128)S(1)}, u32[]{:S(2)}, u32[]{:S(2)}) collective-permute-start(f32[32,16,128]{2,1,0:T(8,128)S(1)} %get-tuple-element.32), channel_id=1, source_target_pairs={{64,0},{128,64},{192,128},{0,192},{65,1},{129,65},{193,129},{1,193... | collective-permute-start | bytes 786440 | tf_op jit(solution)/shard_map/ppermute | solution.py:578
  5.4 0.5 shard_map.59
  5.9 2.5 %collective-permute-start.2 = (f32[48,8,128]{2,1,0:T(8,128)S(1)}, f32[48,8,128]{2,1,0:T(8,128)S(1)}, u32[]{:S(2)}, u32[]{:S(2)}) collective-permute-start(f32[48,8,128]{2,1,0:T(8,128)S(1)} %get-tuple-element.35), channel_id=1, source_target_pairs={{0,8},{8,16},{16,24},{24,32},{32,40},{40,48},{48,56},{56,0},{1,9},... | collective-permute-start | bytes 589832 | tf_op jit(solution)/shard_map/ppermute | solution.py:578
  8.5 0.6 collective-permute-start.3
  9.1 1.6 %collective-permute-done.1.after_ref.x_after = f32[32,16,128]{2,1,0:T(8,128)S(1)} collective-permute-done((f32[32,16,128]{2,1,0:T(8,128)S(1)}, f32[32,16,128]{2,1,0:T(8,128)S(1)}, u32[]{:S(2)}, u32[]{:S(2)}) %collective-permute-start.1) | collective-permute-done | bytes 262176 | tf_op jit(solution)/shard_map/ppermute | solution.py:578
  10.7 3.3 %collective-permute-start.4 = (f32[20,8,128]{2,1,0:T(8,128)S(1)}, f32[20,8,128]{2,1,0:T(8,128)S(1)}, u32[]{:S(2)}, u32[]{:S(2)}) collective-permute-start(f32[20,8,128]{2,1,0:T(8,128)S(1)} %get-tuple-element.37), channel_id=1, source_target_pairs={{0,8},{8,16},{16,24},{24,32},{32,40},{40,48},{48,56},{56,0},{1,9},... | collective-permute-start | bytes 245768 | tf_op jit(solution)/shard_map/ppermute | solution.py:578
  14.1 1.5 %collective-permute-done.4.more_before = f32[20,8,128]{2,1,0:T(8,128)S(1)} collective-permute-done((f32[20,8,128]{2,1,0:T(8,128)S(1)}, f32[20,8,128]{2,1,0:T(8,128)S(1)}, u32[]{:S(2)}, u32[]{:S(2)}) %collective-permute-start.4) | collective-permute-done | bytes 81952 | tf_op jit(solution)/shard_map/ppermute | solution.py:578
  15.5 2.4 %collective-permute-done.5.more_after = f32[20,8,128]{2,1,0:T(8,128)S(1)} collective-permute-done((f32[20,8,128]{2,1,0:T(8,128)S(1)}, f32[20,8,128]{2,1,0:T(8,128)S(1)}, u32[]{:S(2)}, u32[]{:S(2)}) %collective-permute-start.5) | collective-permute-done | bytes 81952 | tf_op jit(solution)/shard_map/ppermute | solution.py:578
  17.9 0.7 %shard_map.61 = (f32[160,8,128]{2,1,0:T(8,128)S(1)}, f32[12,8,128]{2,1,0:T(8,128)S(1)}, f32[12,8,128]{2,1,0:T(8,128)S(1)}) custom-call(f32[32,16,128]{2,1,0:T(8,128)S(1)} %collective-permute-done.before_ref.x_before, f32[32,16,128]{2,1,0:T(8,128)S(1)} %collective-permute-done.1.after_ref.x_after, f32[48,8,128]{2,1,0:T(8,128)S(1)} %collective-permute-done.2.own_before, ...), custom_call_target="tpu_custom_call" | custom-call | flops 1048576 | bytes 1048576 | tf_op jit(solution)/shard_map/pallas_call | solution.py:561
  18.6 1.7 %collective-permute-start.8 = (f32[12,8,128]{2,1,0:T(8,128)S(1)}, f32[12,8,128]{2,1,0:T(8,128)S(1)}, u32[]{:S(2)}, u32[]{:S(2)}) collective-permute-start(f32[12,8,128]{2,1,0:T(8,128)S(1)} %get-tuple-element.42), channel_id=1, source_target_pairs={{0,1},{1,2},{2,3},{3,4},{4,5},{5,6},{6,7},{7,0},{8,9},{9,10},{10,1... | collective-permute-start | bytes 147464 | tf_op jit(solution)/shard_map/ppermute | solution.py:578
  20.3 4.0 %collective-permute-start.9 = (f32[12,8,128]{2,1,0:T(8,128)S(1)}, f32[12,8,128]{2,1,0:T(8,128)S(1)}, u32[]{:S(2)}, u32[]{:S(2)}) collective-permute-start(f32[12,8,128]{2,1,0:T(8,128)S(1)} %get-tuple-element.43), channel_id=1, source_target_pairs={{1,0},{2,1},{3,2},{4,3},{5,4},{6,5},{7,6},{0,7},{9,8},{10,9},{11,1... | collective-permute-start | bytes 147464 | tf_op jit(solution)/shard_map/ppermute | solution.py:578
  24.3 2.7 %collective-permute-start.7 = (f32[3,16,128]{2,1,0:T(8,128)S(1)}, f32[3,16,128]{2,1,0:T(8,128)S(1)}, u32[]{:S(2)}, u32[]{:S(2)}) collective-permute-start(f32[3,16,128]{2,1,0:T(8,128)S(1)} %get-tuple-element.41), channel_id=1, source_target_pairs={{1,0},{2,1},{3,2},{4,3},{5,4},{6,5},{7,6},{0,7},{9,8},{10,9},{11,1... | collective-permute-start | bytes 73736 | tf_op jit(solution)/shard_map/ppermute | solution.py:608
  27.0 1.2 %collective-permute-done.6.own_before = f32[3,16,128]{2,1,0:T(8,128)S(1)} collective-permute-done((f32[3,16,128]{2,1,0:T(8,128)S(1)}, f32[3,16,128]{2,1,0:T(8,128)S(1)}, u32[]{:S(2)}, u32[]{:S(2)}) %collective-permute-start.6) | collective-permute-done | bytes 24608 | tf_op jit(solution)/shard_map/ppermute | solution.py:607
  28.2 1.7 %shard_map.62 = (f32[32,8,128]{2,1,0:T(8,128)S(1)}, f32[32,8,128]{2,1,0:T(8,128)S(1)}, f32[16,24,128]{2,1,0:T(8,128)S(1)}, f32[2,24,128]{2,1,0:T(8,128)S(1)}, f3...) custom-call(f32[4,4,16,128]{3,2,1,0:T(8,128)S(1)} %get-tuple-element, ...), custom_call_target="tpu_custom_call" | custom-call | flops 1048576 | bytes 1048576 | tf_op jit(solution)/shard_map/pallas_call | solution.py:561
  30.0 1.3 %collective-permute-start.10 = (f32[9,24,128]{2,1,0:T(8,128)S(1)}, f32[9,24,128]{2,1,0:T(8,128)S(1)}, u32[]{:S(2)}, u32[]{:S(2)}) collective-permute-start(f32[9,24,128]{2,1,0:T(8,128)S(1)} %get-tuple-element.49), channel_id=1, source_target_pairs={{0,64},{64,128},{128,192},{192,0},{1,65},{65,129},{129,193},{193,1... | collective-permute-start | bytes 331784 | tf_op jit(solution)/shard_map/ppermute | solution.py:578
  31.2 1.6 %collective-permute-start.11 = (f32[9,24,128]{2,1,0:T(8,128)S(1)}, f32[9,24,128]{2,1,0:T(8,128)S(1)}, u32[]{:S(2)}, u32[]{:S(2)}) collective-permute-start(f32[9,24,128]{2,1,0:T(8,128)S(1)} %get-tuple-element.50), channel_id=1, source_target_pairs={{64,0},{128,64},{192,128},{0,192},{65,1},{129,65},{193,129},{1,193... | collective-permute-start | bytes 331784 | tf_op jit(solution)/shard_map/ppermute | solution.py:578
  32.8 0.7 %shard_map.63.before_ref = f32[8,128]{1,0:T(8,128)S(1)} custom-call(f32[8,32,8,128]{3,2,1,0:T(8,128)S(1)} %bitcast.7), custom_call_target="tpu_custom_call" | custom-call | flops 4194304 | bytes 4194304 | tf_op jit(solution)/shard_map/pallas_call | solution.py:561
  33.6 0.5 shard_map.64.sums_in
  34.0 0.8 %collective-permute-done.10.before_ref = f32[9,24,128]{2,1,0:T(8,128)S(1)} collective-permute-done((f32[9,24,128]{2,1,0:T(8,128)S(1)}, f32[9,24,128]{2,1,0:T(8,128)S(1)}, u32[]{:S(2)}, u32[]{:S(2)}) %collective-permute-start.10) | collective-permute-done | bytes 110624 | tf_op jit(solution)/shard_map/ppermute | solution.py:578
  34.8 1.5 %shard_map.65 = (f32[32,8,128]{2,1,0:T(8,128)S(1)}, f32[32,8,128]{2,1,0:T(8,128)S(1)}, f32[256,128]{1,0:T(8,128)S(1)}) custom-call(f32[4,4,4,16,128]{4,3,2,1,0:T(8,128)S(1)} %copy-done.1, f32[32,16,128]{2,1,0:T(8,128)S(1)} %collective-permute-done.before_ref.x_before, f32[32,16,128]{2,1,0:T(8,128)S(1)} %collective-permute-done.1.after_ref.x_after, ...), custom_call_target="tpu_custom_call" | custom-call | flops 1048576 | bytes 1048576 | tf_op jit(solution)/shard_map/pallas_call | solution.py:561
  36.4 26.5 %all_to_all.5 = f32[256,1,128]{2,1,0:T(1,128)S(1)} all-to-all(f32[256,1,128]{2,1,0:T(1,128)S(1)} %bitcast.12), channel_id=1, replica_groups=mesh['gx'=4,'gy'=8,'gz'=8] {'gx','gy','gz'}, dimensions={0} | all-to-all | bytes 262144 | tf_op jit(solution)/shard_map/all_to_all | solution.py:656
  62.8 1.9 %shard_map.66 = (f32[4,32,8,128]{3,2,1,0:T(8,128)}, f32[4,8]{1,0:T(4,128)}, f32[4,4]{1,0:T(4,128)}) custom-call(f32[32,8,128]{2,1,0:T(8,128)S(1)} %bitcast.11, f32[8,32,8,128]{3,2,1,0:T(8,128)S(1)} %bitcast.10, f32[32,8,128]{2,1,0:T(8,128)S(1)} %get-tuple-element.51.v1_ref.refs_0_, f32[32,8,128]{2,1,0:T(8,128)S(1)} %get-tuple-element.52.v2_ref.refs_1_, ...), custom_call_target="tpu_custom_call" | custom-call | flops 1048576 | bytes 1048576 | tf_op jit(solution)/shard_map/pallas_call | solution.py:561
  (14 shorter events, 0.2 us)
Async XLA Ops:
  0.6 4.8 %copy-start.1 = (f32[4,4,4,16,128]{4,3,2,1,0:T(8,128)S(1)}, f32[4,4,4,16,128]{4,3,2,1,0:T(8,128)}, u32[]{:S(2)}) copy-start(f32[4,4,4,16,128]{4,3,2,1,0:T(8,128)} %r_ref.7) | copy-start | bytes 1572868
  2.0 7.1 %collective-permute-start = (f32[32,16,128]{2,1,0:T(8,128)S(1)}, f32[32,16,128]{2,1,0:T(8,128)S(1)}, u32[]{:S(2)}, u32[]{:S(2)}) collective-permute-start(f32[32,16,128]{2,1,0:T(8,128)S(1)} %get-tuple-element.31), channel_id=1, source_target_pairs={{0,64},{64,128},{128,192},{192,0},{1,65},{65,129},{129,193},{193,1... | collective-permute-start | bytes 786440 | tf_op jit(solution)/shard_map/ppermute | solution.py:578
  4.1 6.6 %collective-permute-start.1 = (f32[32,16,128]{2,1,0:T(8,128)S(1)}, f32[32,16,128]{2,1,0:T(8,128)S(1)}, u32[]{:S(2)}, u32[]{:S(2)}) collective-permute-start(f32[32,16,128]{2,1,0:T(8,128)S(1)} %get-tuple-element.32), channel_id=1, source_target_pairs={{64,0},{128,64},{192,128},{0,192},{65,1},{129,65},{193,129},{1,193... | collective-permute-start | bytes 786440 | tf_op jit(solution)/shard_map/ppermute | solution.py:578
  5.9 8.1 %collective-permute-start.2 = (f32[48,8,128]{2,1,0:T(8,128)S(1)}, f32[48,8,128]{2,1,0:T(8,128)S(1)}, u32[]{:S(2)}, u32[]{:S(2)}) collective-permute-start(f32[48,8,128]{2,1,0:T(8,128)S(1)} %get-tuple-element.35), channel_id=1, source_target_pairs={{0,8},{8,16},{16,24},{24,32},{32,40},{40,48},{48,56},{56,0},{1,9},... | collective-permute-start | bytes 589832 | tf_op jit(solution)/shard_map/ppermute | solution.py:578
  8.5 5.6 %collective-permute-start.3 = (f32[48,8,128]{2,1,0:T(8,128)S(1)}, f32[48,8,128]{2,1,0:T(8,128)S(1)}, u32[]{:S(2)}, u32[]{:S(2)}) collective-permute-start(f32[48,8,128]{2,1,0:T(8,128)S(1)} %get-tuple-element.36), channel_id=1, source_target_pairs={{8,0},{16,8},{24,16},{32,24},{40,32},{48,40},{56,48},{0,56},{9,1},... | collective-permute-start | bytes 589832 | tf_op jit(solution)/shard_map/ppermute | solution.py:578
  10.7 4.8 %collective-permute-start.4 = (f32[20,8,128]{2,1,0:T(8,128)S(1)}, f32[20,8,128]{2,1,0:T(8,128)S(1)}, u32[]{:S(2)}, u32[]{:S(2)}) collective-permute-start(f32[20,8,128]{2,1,0:T(8,128)S(1)} %get-tuple-element.37), channel_id=1, source_target_pairs={{0,8},{8,16},{16,24},{24,32},{32,40},{40,48},{48,56},{56,0},{1,9},... | collective-permute-start | bytes 245768 | tf_op jit(solution)/shard_map/ppermute | solution.py:578
  14.0 3.9 %collective-permute-start.5 = (f32[20,8,128]{2,1,0:T(8,128)S(1)}, f32[20,8,128]{2,1,0:T(8,128)S(1)}, u32[]{:S(2)}, u32[]{:S(2)}) collective-permute-start(f32[20,8,128]{2,1,0:T(8,128)S(1)} %get-tuple-element.38), channel_id=1, source_target_pairs={{8,0},{16,8},{24,16},{32,24},{40,32},{48,40},{56,48},{0,56},{9,1},... | collective-permute-start | bytes 245768 | tf_op jit(solution)/shard_map/ppermute | solution.py:578
  18.6 14.2 %copy-start = (f32[8,4,4,16,128]{4,3,2,1,0:T(8,128)S(1)}, f32[8,4,4,16,128]{4,3,2,1,0:T(8,128)}, u32[]{:S(2)}) copy-start(f32[8,4,4,16,128]{4,3,2,1,0:T(8,128)} %q_ref.1) | copy-start | bytes 3145732
  18.6 9.6 %collective-permute-start.8 = (f32[12,8,128]{2,1,0:T(8,128)S(1)}, f32[12,8,128]{2,1,0:T(8,128)S(1)}, u32[]{:S(2)}, u32[]{:S(2)}) collective-permute-start(f32[12,8,128]{2,1,0:T(8,128)S(1)} %get-tuple-element.42), channel_id=1, source_target_pairs={{0,1},{1,2},{2,3},{3,4},{4,5},{5,6},{6,7},{7,0},{8,9},{9,10},{10,1... | collective-permute-start | bytes 147464 | tf_op jit(solution)/shard_map/ppermute | solution.py:578
  20.3 7.9 %collective-permute-start.9 = (f32[12,8,128]{2,1,0:T(8,128)S(1)}, f32[12,8,128]{2,1,0:T(8,128)S(1)}, u32[]{:S(2)}, u32[]{:S(2)}) collective-permute-start(f32[12,8,128]{2,1,0:T(8,128)S(1)} %get-tuple-element.43), channel_id=1, source_target_pairs={{1,0},{2,1},{3,2},{4,3},{5,4},{6,5},{7,6},{0,7},{9,8},{10,9},{11,1... | collective-permute-start | bytes 147464 | tf_op jit(solution)/shard_map/ppermute | solution.py:578
  24.3 3.9 %collective-permute-start.6 = (f32[3,16,128]{2,1,0:T(8,128)S(1)}, f32[3,16,128]{2,1,0:T(8,128)S(1)}, u32[]{:S(2)}, u32[]{:S(2)}) collective-permute-start(f32[3,16,128]{2,1,0:T(8,128)S(1)} %get-tuple-element.40), channel_id=1, source_target_pairs={{0,1},{1,2},{2,3},{3,4},{4,5},{5,6},{6,7},{7,0},{8,9},{9,10},{10,1... | collective-permute-start | bytes 73736 | tf_op jit(solution)/shard_map/ppermute | solution.py:607
  24.3 3.9 %collective-permute-start.7 = (f32[3,16,128]{2,1,0:T(8,128)S(1)}, f32[3,16,128]{2,1,0:T(8,128)S(1)}, u32[]{:S(2)}, u32[]{:S(2)}) collective-permute-start(f32[3,16,128]{2,1,0:T(8,128)S(1)} %get-tuple-element.41), channel_id=1, source_target_pairs={{1,0},{2,1},{3,2},{4,3},{5,4},{6,5},{7,6},{0,7},{9,8},{10,9},{11,1... | collective-permute-start | bytes 73736 | tf_op jit(solution)/shard_map/ppermute | solution.py:608
  30.0 4.9 %collective-permute-start.10 = (f32[9,24,128]{2,1,0:T(8,128)S(1)}, f32[9,24,128]{2,1,0:T(8,128)S(1)}, u32[]{:S(2)}, u32[]{:S(2)}) collective-permute-start(f32[9,24,128]{2,1,0:T(8,128)S(1)} %get-tuple-element.49), channel_id=1, source_target_pairs={{0,64},{64,128},{128,192},{192,0},{1,65},{65,129},{129,193},{193,1... | collective-permute-start | bytes 331784 | tf_op jit(solution)/shard_map/ppermute | solution.py:578
  31.2 3.6 %collective-permute-start.11 = (f32[9,24,128]{2,1,0:T(8,128)S(1)}, f32[9,24,128]{2,1,0:T(8,128)S(1)}, u32[]{:S(2)}, u32[]{:S(2)}) collective-permute-start(f32[9,24,128]{2,1,0:T(8,128)S(1)} %get-tuple-element.50), channel_id=1, source_target_pairs={{64,0},{128,64},{192,128},{0,192},{65,1},{129,65},{193,129},{1,193... | collective-permute-start | bytes 331784 | tf_op jit(solution)/shard_map/ppermute | solution.py:578
where the time goes:
time: 64.9 us; the launch traced here: 64.8 us
  blocking collectives  26.5 us (41%)
  starting transfers between devices  21.1 us (33%)
  Pallas kernels  8.85 us (14%)
  waiting for transfers between devices  7.58 us (12%)
  between operations  0.71 us (1%)
    all_to_all x1, blocking collectives, on_device(): rows = lax.all_to_all(rows.reshape(devices, 1, span_z), AXES, 0, 0)  26.5 us
    ppermute x10, starting transfers between devices, exchange(): return (lax.ppermute(high, axis, up), lax.ppermute(low, axis, down))  18.5 us
    pallas_call x9, Pallas kernels, call(): pl.pallas_call(body, out_shape=[jax.ShapeDtypeStruct(shape, jnp.float32)...  8.85 us
    ppermute x10, waiting for transfers between devices, exchange(): return (lax.ppermute(high, axis, up), lax.ppermute(low, axis, down))  6.37 us
    ppermute x1, starting transfers between devices, on_device(): z_after = lax.ppermute(own[2], 'gz', down)  2.67 us
  transfers between devices with their start and end apart: 12, of which 6 were waited for; matrix products, arithmetic and copies ran while one was open for 0% of the time, Pallas kernels for 3%

commit v1 on v0

--- a/solution.py
+++ b/solution.py
@@ -319,17 +319,74 @@
 CONDUCTS = SPECIES * 25
 
 
-def conduct(d_of, d_side, c_ref, c_side):
+WITHOUT_Z = SPECIES * 13
+
+
+class Conducts:
+    def __init__(self, plain_ref, z_ref):
+        self.plain_ref, self.z_ref = plain_ref, z_ref
+
+    def __getitem__(self, k):
+        return self.plain_ref[k] if k < WITHOUT_Z else self.z_ref[k - WITHOUT_Z]
+
+
+def early_steps(v_ref, d_ref, r_ref, x_before, x_after, edge_ref, v_in, d_in, c_ref, sum_ref, d_edge, v_edge):
+    main_ref = Planes(own_planes(v_ref, d_ref, r_ref, x_before, x_after), edge_ref)
+    mask = masks()
     for s in range(SPECIES):
         for x in V_PLANES:
-            d = d_of(s, x)
+            factor = mask_of(x, mask[0], *mask[2:])
+            v_in[v_at(s, x)] = main_ref[v_at(s, x)] * factor
+            d_in[v_at(s, x)] = main_ref[d_at(s, x)] * factor
+    lane = iota((ROWS, 128), 1)
+    first, final = lane == 0, lane == 127
+    for s in range(SPECIES):
+        for x in V_PLANES:
+            d = d_in[v_at(s, x)]
             if x < V_PLANES[-1]:
-                c_ref[cx_at(s, x)] = 0.5 * (d + d_of(s, x + 1))
+                c_ref[cx_at(s, x)] = 0.5 * (d + d_in[v_at(s, x + 1)])
             if x in R_PLANES:
                 c_ref[cy_at(s, x)] = 0.5 * (d + next_y(d))
-                c_ref[cz_at(s, x)] = 0.5 * (d + next_z(d, d_side[s // 2], slot_of(s, x)))
-                c_ref[back_at(s, x)] = 0.5 * (d + previous_z(d, d_side[s // 2], slot_of(s, x)))
-    edges = columns(R_PLANES, d_of)
+                c_ref[cz_at(s, x)] = jnp.where(final, 0.0, 0.5 * (d + roll(d, -1, 1)))
+                c_ref[back_at(s, x)] = jnp.where(first, 0.0, 0.5 * (d + roll(d, 1, 1)))
+    for x in R_PLANES:
+        here = [v_in[v_at(t, x)] for t in range(SPECIES)]
+        for s in range(SPECIES):
+            v = here[s]
+            value = v * (1.0 - SHIFTS[0])
+            value = value + c_ref[cz_at(s, x)] * (v - roll(v, -1, 1))
+            value = value + c_ref[back_at(s, x)] * (v - roll(v, 1, 1))
+            for t in range(SPECIES):
+                value = value + main_ref[r_at(s, t, x)] * here[t]
+            value = value + c_ref[cx_at(s, x)] * (v - v_in[v_at(s, x + 1)])
+            value = value + c_ref[cx_at(s, x - 1)] * (v - v_in[v_at(s, x - 1)])
+            along = c_ref[cy_at(s, x)] * (v - next_y(v))
+            sum_ref[6 * s + x + 1] = value + (along - roll(along, 1, 0))
+    for half, (d, v) in enumerate(
+        zip(columns(R_PLANES, lambda s, x: d_in[v_at(s, x)]), columns(R_PLANES, lambda s, x: v_in[v_at(s, x)]))
+    ):
+        d_edge[half] = d
+        v_edge[half] = v
+
+
+def end_first_step(v_in, d_in, c_ref, sum_ref, d_side, v_side, z_ref, mask, store):
+    lane = iota((ROWS, 128), 1)
+    first, final = lane == 0, lane == 127
+    for s in range(SPECIES):
+        for x in R_PLANES:
+            place, half, n = slot_of(s, x), s // 2, 6 * s + x + 1
+
+            def beyond(side, place=place, half=half):
+                return jnp.where(final, roll(side[half], 127 - place - DEEP, 1), roll(side[half], 1 - DEEP - place, 1))
+
+            more = jnp.where(first | final, 0.5 * (d_in[v_at(s, x)] + beyond(d_side)), 0.0)
+            z_ref[cz_at(s, x) - WITHOUT_Z] = jnp.where(final, more, c_ref[cz_at(s, x)])
+            z_ref[back_at(s, x) - WITHOUT_Z] = jnp.where(first, more, c_ref[back_at(s, x)])
+            value = sum_ref[n] + more * (v_in[v_at(s, x)] - beyond(v_side))
+            store(s, x, value * (DAMPING * mask_of(x, mask[0], *mask[2:])))
+
+
+def side_conduct(d_side, edges, c_side):
     for half in range(HALVES):
         d = d_side[half]
         c_side[4 * half] = 0.5 * (d + roll(d, -8, 1))
@@ -357,7 +414,11 @@
             store(s, x, value * factor)
     if not sides:
         return None
-    edges = columns(planes, v_of)
+    return side_step(degree, columns(planes, v_of), v_side, side_ref, c_side, mask)
+
+
+def side_step(degree, edges, v_side, side_ref, c_side, mask):
+    lane = iota((ROWS, 128), 1)
     both = []
     for half in range(HALVES):
         other = roll(v_side[half], 64, 1)
@@ -379,28 +440,26 @@
     return result
 
 
+FACE_EDGES = SPECIES * WIDE * 2
+FACE_SIDE = FACE_EDGES + SPECIES
+FACE_TILES = FACE_SIDE + 3
+
+
 def put_own(out_ref, s, x, value):
     out_ref[8 * s + 2 * x] = value[:8]
     out_ref[8 * s + 2 * x + 1] = value[8:16]
 
 
-def first_steps(v_ref, d_ref, r_ref, x_before, x_after, edge_ref, own_before, own_after, more_before, more_after, v1_ref, v2_ref, wide_ref, wide_side, low_ref, high_ref, side_ref, c_ref, c_side, v_in, v_mid):
-    main_ref = Planes(own_planes(v_ref, d_ref, r_ref, x_before, x_after), edge_ref)
+def first_steps(r_ref, x_before, x_after, edge_ref, v_in, d_in, c_early, sum_ref, d_edge, v_edge, own_before, own_after, more_before, more_after, v1_ref, v2_ref, wide_ref, wide_side, low_ref, high_ref, side_ref, z_ref, c_side, v_mid):
+    main_ref = Planes(own_planes(None, None, r_ref, x_before, x_after), edge_ref)
     lane = iota((ROWS, 128), 1)
     for side in range(SIDES):
         side_ref[side] = unpack_z(side, own_before, own_after, more_before, more_after)
     mask = masks()
-
-    def inside(plane, x):
-        return main_ref[plane] * mask_of(x, mask[0], *mask[2:])
-
     v_side = [side_ref[half] * mask[1] for half in range(HALVES)]
     d_side = [side_ref[HALVES + half] * mask[1] for half in range(HALVES)]
-    for s in range(SPECIES):
-        for x in V_PLANES:
-            v_mid[v_at(s, x)] = inside(d_at(s, x), x)
-            v_in[v_at(s, x)] = inside(v_at(s, x), x)
-    conduct(lambda s, x: v_mid[v_at(s, x)], d_side, c_ref, c_side)
+    side_conduct(d_side, d_edge, c_side)
+    c_ref = Conducts(c_early, z_ref)
 
     def store_mid(s, x, value):
         v_mid[v_at(s, x)] = value
@@ -412,28 +471,42 @@
         put_own(v2_ref, s, x, value)
 
     more = (main_ref, side_ref, c_ref, c_side, mask)
-    v_side = step(0, R_PLANES, lambda s, x: v_in[v_at(s, x)], v_side, *more, store_mid)
+    end_first_step(v_in, d_in, c_early, sum_ref, d_side, v_side, z_ref, mask, store_mid)
+    v_side = side_step(0, v_edge, v_side, side_ref, c_side, mask)
     v_side = step(1, range(4), lambda s, x: v_mid[v_at(s, x)], v_side, *more, store_wide)
     for half in range(HALVES):
         wide_side[half] = v_side[half]
     slot = lane // 8 % 8
+    row = iota((8, 128), 0)
+    near = (row < 2) | (row >= 6)
     for face, start, shift in ((low_ref, 0, -16), (high_ref, 4 - WIDE, 16)):
         for s in range(SPECIES):
+            values = [wide_ref[4 * s + start + n] for n in range(WIDE)]
             for n in range(WIDE):
-                face[s * WIDE + n] = wide_ref[4 * s + start + n]
+                face[(s * WIDE + n) * 2] = values[n][:8]
+                face[(s * WIDE + n) * 2 + 1] = values[n][8:16]
+            face[FACE_EDGES + s] = jnp.where(near, values[0][16:], roll(values[1][16:], DEEP, 0))
         kept = (slot >= start + WIDE) & (slot < start + 2 * WIDE)
-        face[SPECIES * WIDE] = jnp.where(kept, v_side[0], roll(v_side[1], shift, 1))
-
-
-def last_steps(r_ref, x_before, x_after, edge_ref, side_ref, c_ref, c_side, wide_ref, wide_side, before_ref, after_ref, q_ref, v1_ref, v2_ref, sums_in, v3_ref, v4_ref, sums_ref, v_in, v_mid):
+        packed = jnp.where(kept, v_side[0], roll(v_side[1], shift, 1))
+        for n in range(3):
+            face[FACE_SIDE + n] = packed[8 * n : 8 * n + 8]
+
+
+def last_steps(r_ref, x_before, x_after, edge_ref, side_ref, c_early, z_ref, c_side, wide_ref, wide_side, before_ref, after_ref, q_ref, v1_ref, v2_ref, sums_in, v3_ref, v4_ref, sums_ref, v_in, v_mid):
     main_ref = Planes(own_planes(None, None, r_ref, x_before, x_after), edge_ref)
+    c_ref = Conducts(c_early, z_ref)
     mask = masks()
     for s in range(SPECIES):
         for face, start, factor in ((before_ref, -WIDE, mask[2]), (after_ref, 4, mask[3])):
             for n in range(WIDE):
-                v_in[v_at(s, start + n)] = face[s * WIDE + n] * factor
+                k = (s * WIDE + n) * 2
+                value = jnp.concatenate([face[k], face[k + 1], roll(face[FACE_EDGES + s], DEEP * n, 0)], 0)
+                v_in[v_at(s, start + n)] = value * factor
     slot = iota((ROWS, 128), 1) // 8 % 8
-    before, after = before_ref[SPECIES * WIDE] * mask[2], after_ref[SPECIES * WIDE] * mask[3]
+    before, after = (
+        jnp.concatenate([face[FACE_SIDE + n] for n in range(3)], 0) * factor
+        for face, factor in ((before_ref, mask[2]), (after_ref, mask[3]))
+    )
     v_side = []
     for half in range(HALVES):
         value = jnp.where(slot < WIDE, roll(before, -32 - 16 * half, 1), wide_side[half])
@@ -616,18 +689,27 @@
     basis = earlier_basis.reshape(EARLIER, tiles, 8, span_z)
     (sums,) = call(earlier_products, [(8, span_z)], 4 << 20, basis)
     own = (tiles, 8, span_z)
-    scratch = [pltpu.VMEM((D_BASE, ROWS, span_z), jnp.float32)] * 2
-    several = [
-        (count, ROWS, span_z)
-        for count in (SPECIES * span_x, HALVES, SPECIES * WIDE + 1, SPECIES * WIDE + 1, SIDES, CONDUCTS, 4 * HALVES)
-    ]
-    v1, v2, wide, wide_side, low, high, side, conducts, side_conducts = call(
-        first_steps,
-        [own, own] + several,
+    plane = (ROWS, span_z)
+    early = call(
+        early_steps,
+        [(count,) + plane for count in (D_BASE, D_BASE, CONDUCTS, SPECIES * len(R_PLANES), HALVES, HALVES)],
         1 << 20,
         *kept,
         *x_halos,
         edge,
+    )
+    scratch = [pltpu.VMEM((D_BASE,) + plane, jnp.float32)]
+    face = (FACE_TILES, 8, span_z)
+    several = [(count,) + plane for count in (SPECIES * span_x, HALVES)] + [face, face]
+    several += [(count,) + plane for count in (SIDES, CONDUCTS - WITHOUT_Z, 4 * HALVES)]
+    v1, v2, wide, wide_side, low, high, side, z_conducts, side_conducts = call(
+        first_steps,
+        [own, own] + several,
+        1 << 20,
+        reaction,
+        *x_halos,
+        edge,
+        *early,
         *z_own,
         *z_more,
         scratch_shapes=scratch,
@@ -642,7 +724,8 @@
         *x_halos,
         edge,
         side,
-        conducts,
+        early[2],
+        z_conducts,
         side_conducts,
         wide,
         wide_side,
@@ -651,7 +734,7 @@
         v1,
         v2,
         sums,
-        scratch_shapes=scratch,
+        scratch_shapes=scratch * 2,
     )
     rows = lax.all_to_all(rows.reshape(devices, 1, span_z), AXES, 0, 0)
     new, coeff, triangle = call(

time: 64.9 us -> 64.1 us (0.988)
  waiting for transfers between devices: 7.58 us -> 6.75 us
    ppermute x1, waiting for transfers between devices: 1.21 us -> 0.55 us  [on_device(): z_before = lax.ppermute(own[3], 'gz', up)]
    pallas_call x9 -> x10, Pallas kernels: 8.85 us -> 8.89 us  [call(): pl.pallas_call(body, out_shape=[jax.ShapeDtypeStruct(shape, jnp.float32)...]
  transfers between devices with their start and end apart: 12 -> 12, of which waited for: 6 -> 6; matrix products, arithmetic and copies ran while one was open for 0% -> 0% of each run, Pallas kernels for 3% -> 4%
where the time goes in v1:
time: 64.1 us; the launch traced here: 64 us
  blocking collectives  26.5 us (41%)
  starting transfers between devices  21.1 us (33%)
  Pallas kernels  8.89 us (14%)
  waiting for transfers between devices  6.75 us (11%)
  between operations  0.72 us (1%)
    all_to_all x1, blocking collectives, on_device(): rows = lax.all_to_all(rows.reshape(devices, 1, span_z), AXES, 0, 0)  26.5 us
    ppermute x10, starting transfers between devices, exchange(): return (lax.ppermute(high, axis, up), lax.ppermute(low, axis, down))  18.5 us
    pallas_call x10, Pallas kernels, call(): pl.pallas_call(body, out_shape=[jax.ShapeDtypeStruct(shape, jnp.float32)...  8.89 us
    ppermute x10, waiting for transfers between devices, exchange(): return (lax.ppermute(high, axis, up), lax.ppermute(low, axis, down))  6.19 us
    ppermute x1, starting transfers between devices, on_device(): z_after = lax.ppermute(own[2], 'gz', down)  2.67 us
  transfers between devices with their start and end apart: 12, of which 6 were waited for; matrix products, arithmetic and copies ran while one was open for 0% of the time, Pallas kernels for 4%

profile of v1, /device:TPU:1, one launch (start us, length us, event | category | flops | bytes accessed | tf_op | source)
XLA Modules:
  0.0 64.0 jit_solution(2543737427211594893)
XLA Ops:
  0.6 1.3 %shard_map.58 = (f32[32,16,128]{2,1,0:T(8,128)S(1)}, f32[32,16,128]{2,1,0:T(8,128)S(1)}, f32[4,4,16,128]{3,2,1,0:T(8,128)S(1)}, f32[4,4,16,128]{3,2,1,0:T(8,128)S(1)}) custom-call(f32[8,4,4,16,128]{4,3,2,1,0:T(8,128)} %q_ref.1, f32[4,4,16,128]{3,2,1,0:T(8,128)} %d_ref.1, f32[4,4,4,16,128]{4,3,2,1,0:T(8,128)} %r_ref.9), custom_call_target="tpu_custom_call" | custom-call | flops 1048576 | bytes 1048576 | tf_op jit(solution)/shard_map/pallas_call | solution.py:634
  2.0 2.1 %collective-permute-start = (f32[32,16,128]{2,1,0:T(8,128)S(1)}, f32[32,16,128]{2,1,0:T(8,128)S(1)}, u32[]{:S(2)}, u32[]{:S(2)}) collective-permute-start(f32[32,16,128]{2,1,0:T(8,128)S(1)} %get-tuple-element.37), channel_id=1, source_target_pairs={{0,64},{64,128},{128,192},{192,0},{1,65},{65,129},{129,193},{193,1... | collective-permute-start | bytes 786440 | tf_op jit(solution)/shard_map/ppermute | solution.py:651
  4.1 1.4 %collective-permute-start.1 = (f32[32,16,128]{2,1,0:T(8,128)S(1)}, f32[32,16,128]{2,1,0:T(8,128)S(1)}, u32[]{:S(2)}, u32[]{:S(2)}) collective-permute-start(f32[32,16,128]{2,1,0:T(8,128)S(1)} %get-tuple-element.38), channel_id=1, source_target_pairs={{64,0},{128,64},{192,128},{0,192},{65,1},{129,65},{193,129},{1,193... | collective-permute-start | bytes 786440 | tf_op jit(solution)/shard_map/ppermute | solution.py:651
  5.4 0.5 shard_map.59
  5.9 2.5 %collective-permute-start.2 = (f32[48,8,128]{2,1,0:T(8,128)S(1)}, f32[48,8,128]{2,1,0:T(8,128)S(1)}, u32[]{:S(2)}, u32[]{:S(2)}) collective-permute-start(f32[48,8,128]{2,1,0:T(8,128)S(1)} %get-tuple-element.41), channel_id=1, source_target_pairs={{0,8},{8,16},{16,24},{24,32},{32,40},{40,48},{48,56},{56,0},{1,9},... | collective-permute-start | bytes 589832 | tf_op jit(solution)/shard_map/ppermute | solution.py:651
  8.5 0.6 collective-permute-start.3
  9.1 1.6 %collective-permute-done.1.after_ref.x_after = f32[32,16,128]{2,1,0:T(8,128)S(1)} collective-permute-done((f32[32,16,128]{2,1,0:T(8,128)S(1)}, f32[32,16,128]{2,1,0:T(8,128)S(1)}, u32[]{:S(2)}, u32[]{:S(2)}) %collective-permute-start.1) | collective-permute-done | bytes 262176 | tf_op jit(solution)/shard_map/ppermute | solution.py:651
  10.7 3.3 %collective-permute-start.4 = (f32[20,8,128]{2,1,0:T(8,128)S(1)}, f32[20,8,128]{2,1,0:T(8,128)S(1)}, u32[]{:S(2)}, u32[]{:S(2)}) collective-permute-start(f32[20,8,128]{2,1,0:T(8,128)S(1)} %get-tuple-element.43), channel_id=1, source_target_pairs={{0,8},{8,16},{16,24},{24,32},{32,40},{40,48},{48,56},{56,0},{1,9},... | collective-permute-start | bytes 245768 | tf_op jit(solution)/shard_map/ppermute | solution.py:651
  14.1 1.5 %collective-permute-done.4.more_before = f32[20,8,128]{2,1,0:T(8,128)S(1)} collective-permute-done((f32[20,8,128]{2,1,0:T(8,128)S(1)}, f32[20,8,128]{2,1,0:T(8,128)S(1)}, u32[]{:S(2)}, u32[]{:S(2)}) %collective-permute-start.4) | collective-permute-done | bytes 81952 | tf_op jit(solution)/shard_map/ppermute | solution.py:651
  15.5 2.4 %collective-permute-done.5.more_after = f32[20,8,128]{2,1,0:T(8,128)S(1)} collective-permute-done((f32[20,8,128]{2,1,0:T(8,128)S(1)}, f32[20,8,128]{2,1,0:T(8,128)S(1)}, u32[]{:S(2)}, u32[]{:S(2)}) %collective-permute-start.5) | collective-permute-done | bytes 81952 | tf_op jit(solution)/shard_map/ppermute | solution.py:651
  17.9 0.7 %shard_map.61 = (f32[160,8,128]{2,1,0:T(8,128)S(1)}, f32[12,8,128]{2,1,0:T(8,128)S(1)}, f32[12,8,128]{2,1,0:T(8,128)S(1)}) custom-call(f32[32,16,128]{2,1,0:T(8,128)S(1)} %collective-permute-done.before_ref.x_before, f32[32,16,128]{2,1,0:T(8,128)S(1)} %collective-permute-done.1.after_ref.x_after, f32[48,8,128]{2,1,0:T(8,128)S(1)} %collective-permute-done.2.own_before, ...), custom_call_target="tpu_custom_call" | custom-call | flops 1048576 | bytes 1048576 | tf_op jit(solution)/shard_map/pallas_call | solution.py:634
  18.6 1.7 %collective-permute-start.8 = (f32[12,8,128]{2,1,0:T(8,128)S(1)}, f32[12,8,128]{2,1,0:T(8,128)S(1)}, u32[]{:S(2)}, u32[]{:S(2)}) collective-permute-start(f32[12,8,128]{2,1,0:T(8,128)S(1)} %get-tuple-element.54), channel_id=1, source_target_pairs={{0,1},{1,2},{2,3},{3,4},{4,5},{5,6},{6,7},{7,0},{8,9},{9,10},{10,1... | collective-permute-start | bytes 147464 | tf_op jit(solution)/shard_map/ppermute | solution.py:651
  20.3 4.0 %collective-permute-start.9 = (f32[12,8,128]{2,1,0:T(8,128)S(1)}, f32[12,8,128]{2,1,0:T(8,128)S(1)}, u32[]{:S(2)}, u32[]{:S(2)}) collective-permute-start(f32[12,8,128]{2,1,0:T(8,128)S(1)} %get-tuple-element.55), channel_id=1, source_target_pairs={{1,0},{2,1},{3,2},{4,3},{5,4},{6,5},{7,6},{0,7},{9,8},{10,9},{11,1... | collective-permute-start | bytes 147464 | tf_op jit(solution)/shard_map/ppermute | solution.py:651
  24.3 2.7 %collective-permute-start.7 = (f32[3,16,128]{2,1,0:T(8,128)S(1)}, f32[3,16,128]{2,1,0:T(8,128)S(1)}, u32[]{:S(2)}, u32[]{:S(2)}) collective-permute-start(f32[3,16,128]{2,1,0:T(8,128)S(1)} %get-tuple-element.53), channel_id=1, source_target_pairs={{1,0},{2,1},{3,2},{4,3},{5,4},{6,5},{7,6},{0,7},{9,8},{10,9},{11,1... | collective-permute-start | bytes 73736 | tf_op jit(solution)/shard_map/ppermute | solution.py:681
  27.0 0.7 %shard_map.62 = (f32[32,24,128]{2,1,0:T(8,128)S(1)}, f32[32,24,128]{2,1,0:T(8,128)S(1)}, f32[100,24,128]{2,1,0:T(8,128)S(1)}, f32[24,24,128]{2,1,0:T(8,128)S(1)}...) custom-call(f32[4,4,16,128]{3,2,1,0:T(8,128)S(1)} %get-tuple-element.39.v_ref, ...), custom_call_target="tpu_custom_call" | custom-call | flops 1048576 | bytes 1048576 | tf_op jit(solution)/shard_map/pallas_call | solution.py:634
  27.7 0.6 collective-permute-done.6.own_before
  28.2 1.1 %shard_map.63 = (f32[32,8,128]{2,1,0:T(8,128)S(1)}, f32[32,8,128]{2,1,0:T(8,128)S(1)}, f32[16,24,128]{2,1,0:T(8,128)S(1)}, f32[2,24,128]{2,1,0:T(8,128)S(1)}, f3...) custom-call(f32[4,4,4,16,128]{4,3,2,1,0:T(8,128)S(1)} %copy-done.1, ...), custom_call_target="tpu_custom_call" | custom-call | flops 1048576 | bytes 1048576 | tf_op jit(solution)/shard_map/pallas_call | solution.py:634
  29.3 1.3 %collective-permute-start.10 = (f32[23,8,128]{2,1,0:T(8,128)S(1)}, f32[23,8,128]{2,1,0:T(8,128)S(1)}, u32[]{:S(2)}, u32[]{:S(2)}) collective-permute-start(f32[23,8,128]{2,1,0:T(8,128)S(1)} %get-tuple-element.61), channel_id=1, source_target_pairs={{0,64},{64,128},{128,192},{192,0},{1,65},{65,129},{129,193},{193,1... | collective-permute-start | bytes 282632 | tf_op jit(solution)/shard_map/ppermute | solution.py:651
  30.6 1.6 %collective-permute-start.11 = (f32[23,8,128]{2,1,0:T(8,128)S(1)}, f32[23,8,128]{2,1,0:T(8,128)S(1)}, u32[]{:S(2)}, u32[]{:S(2)}) collective-permute-start(f32[23,8,128]{2,1,0:T(8,128)S(1)} %get-tuple-element.62), channel_id=1, source_target_pairs={{64,0},{128,64},{192,128},{0,192},{65,1},{129,65},{193,129},{1,193... | collective-permute-start | bytes 282632 | tf_op jit(solution)/shard_map/ppermute | solution.py:651
  32.2 0.7 %shard_map.64.before_ref = f32[8,128]{1,0:T(8,128)S(1)} custom-call(f32[8,32,8,128]{3,2,1,0:T(8,128)S(1)} %bitcast.7), custom_call_target="tpu_custom_call" | custom-call | flops 4194304 | bytes 4194304 | tf_op jit(solution)/shard_map/pallas_call | solution.py:634
  33.4 0.6 %collective-permute-done.10.before_ref = f32[23,8,128]{2,1,0:T(8,128)S(1)} collective-permute-done((f32[23,8,128]{2,1,0:T(8,128)S(1)}, f32[23,8,128]{2,1,0:T(8,128)S(1)}, u32[]{:S(2)}, u32[]{:S(2)}) %collective-permute-start.10) | collective-permute-done | bytes 94240 | tf_op jit(solution)/shard_map/ppermute | solution.py:651
  34.0 1.5 %shard_map.66 = (f32[32,8,128]{2,1,0:T(8,128)S(1)}, f32[32,8,128]{2,1,0:T(8,128)S(1)}, f32[256,128]{1,0:T(8,128)S(1)}) custom-call(f32[4,4,4,16,128]{4,3,2,1,0:T(8,128)S(1)} %copy-done.1, f32[32,16,128]{2,1,0:T(8,128)S(1)} %collective-permute-done.before_ref.x_before, f32[32,16,128]{2,1,0:T(8,128)S(1)} %collective-permute-done.1.after_ref.x_after, ...), custom_call_target="tpu_custom_call" | custom-call | flops 1048576 | bytes 1048576 | tf_op jit(solution)/shard_map/pallas_call | solution.py:634
  35.6 26.5 %all_to_all.5 = f32[256,1,128]{2,1,0:T(1,128)S(1)} all-to-all(f32[256,1,128]{2,1,0:T(1,128)S(1)} %bitcast.12), channel_id=1, replica_groups=mesh['gx'=4,'gy'=8,'gz'=8] {'gx','gy','gz'}, dimensions={0} | all-to-all | bytes 262144 | tf_op jit(solution)/shard_map/all_to_all | solution.py:739
  62.0 1.9 %shard_map.67 = (f32[4,32,8,128]{3,2,1,0:T(8,128)}, f32[4,8]{1,0:T(4,128)}, f32[4,4]{1,0:T(4,128)}) custom-call(f32[32,8,128]{2,1,0:T(8,128)S(1)} %bitcast.11, f32[8,32,8,128]{3,2,1,0:T(8,128)S(1)} %bitcast.10, f32[32,8,128]{2,1,0:T(8,128)S(1)} %get-tuple-element.63.v1_ref.refs_0_, f32[32,8,128]{2,1,0:T(8,128)S(1)} %get-tuple-element.64.v2_ref.refs_1_, ...), custom_call_target="tpu_custom_call" | custom-call | flops 1048576 | bytes 1048576 | tf_op jit(solution)/shard_map/pallas_call | solution.py:634
  (15 shorter events, 0.6 us)
Async XLA Ops:
  0.6 4.8 %copy-start.1 = (f32[4,4,4,16,128]{4,3,2,1,0:T(8,128)S(1)}, f32[4,4,4,16,128]{4,3,2,1,0:T(8,128)}, u32[]{:S(2)}) copy-start(f32[4,4,4,16,128]{4,3,2,1,0:T(8,128)} %r_ref.9) | copy-start | bytes 1572868
  2.0 7.1 %collective-permute-start = (f32[32,16,128]{2,1,0:T(8,128)S(1)}, f32[32,16,128]{2,1,0:T(8,128)S(1)}, u32[]{:S(2)}, u32[]{:S(2)}) collective-permute-start(f32[32,16,128]{2,1,0:T(8,128)S(1)} %get-tuple-element.37), channel_id=1, source_target_pairs={{0,64},{64,128},{128,192},{192,0},{1,65},{65,129},{129,193},{193,1... | collective-permute-start | bytes 786440 | tf_op jit(solution)/shard_map/ppermute | solution.py:651
  4.1 6.6 %collective-permute-start.1 = (f32[32,16,128]{2,1,0:T(8,128)S(1)}, f32[32,16,128]{2,1,0:T(8,128)S(1)}, u32[]{:S(2)}, u32[]{:S(2)}) collective-permute-start(f32[32,16,128]{2,1,0:T(8,128)S(1)} %get-tuple-element.38), channel_id=1, source_target_pairs={{64,0},{128,64},{192,128},{0,192},{65,1},{129,65},{193,129},{1,193... | collective-permute-start | bytes 786440 | tf_op jit(solution)/shard_map/ppermute | solution.py:651
  5.9 8.1 %collective-permute-start.2 = (f32[48,8,128]{2,1,0:T(8,128)S(1)}, f32[48,8,128]{2,1,0:T(8,128)S(1)}, u32[]{:S(2)}, u32[]{:S(2)}) collective-permute-start(f32[48,8,128]{2,1,0:T(8,128)S(1)} %get-tuple-element.41), channel_id=1, source_target_pairs={{0,8},{8,16},{16,24},{24,32},{32,40},{40,48},{48,56},{56,0},{1,9},... | collective-permute-start | bytes 589832 | tf_op jit(solution)/shard_map/ppermute | solution.py:651
  8.5 5.6 %collective-permute-start.3 = (f32[48,8,128]{2,1,0:T(8,128)S(1)}, f32[48,8,128]{2,1,0:T(8,128)S(1)}, u32[]{:S(2)}, u32[]{:S(2)}) collective-permute-start(f32[48,8,128]{2,1,0:T(8,128)S(1)} %get-tuple-element.42), channel_id=1, source_target_pairs={{8,0},{16,8},{24,16},{32,24},{40,32},{48,40},{56,48},{0,56},{9,1},... | collective-permute-start | bytes 589832 | tf_op jit(solution)/shard_map/ppermute | solution.py:651
  10.7 4.8 %collective-permute-start.4 = (f32[20,8,128]{2,1,0:T(8,128)S(1)}, f32[20,8,128]{2,1,0:T(8,128)S(1)}, u32[]{:S(2)}, u32[]{:S(2)}) collective-permute-start(f32[20,8,128]{2,1,0:T(8,128)S(1)} %get-tuple-element.43), channel_id=1, source_target_pairs={{0,8},{8,16},{16,24},{24,32},{32,40},{40,48},{48,56},{56,0},{1,9},... | collective-permute-start | bytes 245768 | tf_op jit(solution)/shard_map/ppermute | solution.py:651
  14.0 3.9 %collective-permute-start.5 = (f32[20,8,128]{2,1,0:T(8,128)S(1)}, f32[20,8,128]{2,1,0:T(8,128)S(1)}, u32[]{:S(2)}, u32[]{:S(2)}) collective-permute-start(f32[20,8,128]{2,1,0:T(8,128)S(1)} %get-tuple-element.44), channel_id=1, source_target_pairs={{8,0},{16,8},{24,16},{32,24},{40,32},{48,40},{56,48},{0,56},{9,1},... | collective-permute-start | bytes 245768 | tf_op jit(solution)/shard_map/ppermute | solution.py:651
  18.6 9.6 %collective-permute-start.8 = (f32[12,8,128]{2,1,0:T(8,128)S(1)}, f32[12,8,128]{2,1,0:T(8,128)S(1)}, u32[]{:S(2)}, u32[]{:S(2)}) collective-permute-start(f32[12,8,128]{2,1,0:T(8,128)S(1)} %get-tuple-element.54), channel_id=1, source_target_pairs={{0,1},{1,2},{2,3},{3,4},{4,5},{5,6},{6,7},{7,0},{8,9},{9,10},{10,1... | collective-permute-start | bytes 147464 | tf_op jit(solution)/shard_map/ppermute | solution.py:651
  20.3 7.9 %collective-permute-start.9 = (f32[12,8,128]{2,1,0:T(8,128)S(1)}, f32[12,8,128]{2,1,0:T(8,128)S(1)}, u32[]{:S(2)}, u32[]{:S(2)}) collective-permute-start(f32[12,8,128]{2,1,0:T(8,128)S(1)} %get-tuple-element.55), channel_id=1, source_target_pairs={{1,0},{2,1},{3,2},{4,3},{5,4},{6,5},{7,6},{0,7},{9,8},{10,9},{11,1... | collective-permute-start | bytes 147464 | tf_op jit(solution)/shard_map/ppermute | solution.py:651
  24.3 3.9 %collective-permute-start.6 = (f32[3,16,128]{2,1,0:T(8,128)S(1)}, f32[3,16,128]{2,1,0:T(8,128)S(1)}, u32[]{:S(2)}, u32[]{:S(2)}) collective-permute-start(f32[3,16,128]{2,1,0:T(8,128)S(1)} %get-tuple-element.52), channel_id=1, source_target_pairs={{0,1},{1,2},{2,3},{3,4},{4,5},{5,6},{6,7},{7,0},{8,9},{9,10},{10,1... | collective-permute-start | bytes 73736 | tf_op jit(solution)/shard_map/ppermute | solution.py:680
  24.3 3.9 %collective-permute-start.7 = (f32[3,16,128]{2,1,0:T(8,128)S(1)}, f32[3,16,128]{2,1,0:T(8,128)S(1)}, u32[]{:S(2)}, u32[]{:S(2)}) collective-permute-start(f32[3,16,128]{2,1,0:T(8,128)S(1)} %get-tuple-element.53), channel_id=1, source_target_pairs={{1,0},{2,1},{3,2},{4,3},{5,4},{6,5},{7,6},{0,7},{9,8},{10,9},{11,1... | collective-permute-start | bytes 73736 | tf_op jit(solution)/shard_map/ppermute | solution.py:681
  28.2 3.9 %copy-start = (f32[8,4,4,16,128]{4,3,2,1,0:T(8,128)S(1)}, f32[8,4,4,16,128]{4,3,2,1,0:T(8,128)}, u32[]{:S(2)}) copy-start(f32[8,4,4,16,128]{4,3,2,1,0:T(8,128)} %q_ref.1) | copy-start | bytes 3145732
  29.3 4.7 %collective-permute-start.10 = (f32[23,8,128]{2,1,0:T(8,128)S(1)}, f32[23,8,128]{2,1,0:T(8,128)S(1)}, u32[]{:S(2)}, u32[]{:S(2)}) collective-permute-start(f32[23,8,128]{2,1,0:T(8,128)S(1)} %get-tuple-element.61), channel_id=1, source_target_pairs={{0,64},{64,128},{128,192},{192,0},{1,65},{65,129},{129,193},{193,1... | collective-permute-start | bytes 282632 | tf_op jit(solution)/shard_map/ppermute | solution.py:651
  30.6 3.4 %collective-permute-start.11 = (f32[23,8,128]{2,1,0:T(8,128)S(1)}, f32[23,8,128]{2,1,0:T(8,128)S(1)}, u32[]{:S(2)}, u32[]{:S(2)}) collective-permute-start(f32[23,8,128]{2,1,0:T(8,128)S(1)} %get-tuple-element.62), channel_id=1, source_target_pairs={{64,0},{128,64},{192,128},{0,192},{65,1},{129,65},{193,129},{1,193... | collective-permute-start | bytes 282632 | tf_op jit(solution)/shard_map/ppermute | solution.py:651

commit v2 on v1

--- a/solution.py
+++ b/solution.py
@@ -190,10 +190,18 @@
     return low, high
 
 
-def more_z_faces(x_before, x_after, own_before, own_after, more_before, more_after, edge_ref, low_ref, high_ref):
+def is_own(plane):
+    return Y_PLACES[plane][0] == 0
+
+
+def y_edge(plane, before_ref, after_ref):
+    _, tile, place, rows = Y_PLACES[plane]
+    after = roll(after_ref[tile], -rows * place, 0)
+    return jnp.where(iota((8, 128), 0) < DEEP, after, roll(before_ref[tile], 8 - rows - rows * place, 0))
+
+
+def some_z_faces(x_before, x_after, y_before, y_after, edge_ref, low_ref, high_ref):
     planes = own_planes(None, None, None, x_before, x_after)
-    top = iota((8, 128), 0) < DEEP
-    befores, afters = (own_before, more_before), (own_after, more_after)
     for block, found in enumerate(z_groups(False)):
         low, high = pack_z(found, lambda plane: planes[plane](pl.ds(0, 16)), 16)
         for half in range(2):
@@ -201,14 +209,25 @@
             high_ref[2 * block + half] = high[8 * half : 8 * half + 8]
 
     def value_of(plane):
-        message, tile, place, rows = Y_PLACES[plane]
-        after = roll(afters[message][tile], -rows * place, 0)
-        before = roll(befores[message][tile], 8 - rows - rows * place, 0)
-        edge_ref[plane] = jnp.where(top, after, before)
+        edge_ref[plane] = y_edge(plane, y_before, y_after)
         return edge_ref[plane]
 
     for block, found in enumerate(z_edge_groups()):
+        found = [(plane, k) for plane, k in found if is_own(plane)]
         low_ref[BLOCKS + block], high_ref[BLOCKS + block] = pack_z(found, value_of, 8)
+
+
+def more_z_faces(y_before, y_after, some_low, some_high, edge_ref, low_ref, high_ref):
+    def value_of(plane):
+        edge_ref[plane] = y_edge(plane, y_before, y_after)
+        return edge_ref[plane]
+
+    for block, found in enumerate(z_edge_groups()):
+        low_ref[block], high_ref[block] = some_low[block], some_high[block]
+        found = [(plane, k) for plane, k in found if not is_own(plane)]
+        low, high = pack_z(found, value_of, 8)
+        low_ref[BLOCKS + block] = some_low[BLOCKS + block] + low
+        high_ref[BLOCKS + block] = some_high[BLOCKS + block] + high
 
 
 def unpack_z(side, own_before, own_after, more_before, more_after):
@@ -232,11 +251,12 @@
 
 
 class Planes:
-    def __init__(self, planes, edge_ref):
-        self.planes, self.edge_ref = planes, edge_ref
+    def __init__(self, planes, edge_own, edge_more):
+        self.planes, self.edge_own, self.edge_more = planes, edge_own, edge_more
 
     def __getitem__(self, plane):
-        return jnp.concatenate([self.planes[plane](pl.ds(0, 16)), self.edge_ref[plane]], 0)
+        edge_ref = self.edge_own if is_own(plane) else self.edge_more
+        return jnp.concatenate([self.planes[plane](pl.ds(0, 16)), edge_ref[plane]], 0)
 
 
 def masks():
@@ -330,8 +350,8 @@
         return self.plain_ref[k] if k < WITHOUT_Z else self.z_ref[k - WITHOUT_Z]
 
 
-def early_steps(v_ref, d_ref, r_ref, x_before, x_after, edge_ref, v_in, d_in, c_ref, sum_ref, d_edge, v_edge):
-    main_ref = Planes(own_planes(v_ref, d_ref, r_ref, x_before, x_after), edge_ref)
+def early_steps(v_ref, d_ref, r_ref, x_before, x_after, edge_own, edge_more, v_in, d_in, c_ref, sum_ref, d_edge, v_edge):
+    main_ref = Planes(own_planes(v_ref, d_ref, r_ref, x_before, x_after), edge_own, edge_more)
     mask = masks()
     for s in range(SPECIES):
         for x in V_PLANES:
@@ -395,23 +415,26 @@
         c_side[4 * half + 3] = 0.5 * (d + side_previous_z(d, edges[half]))
 
 
+def plane_sum(degree, s, x, v_of, v_side, main_ref, c_ref, before=True, after=True):
+    half, place, v = s // 2, slot_of(s, x), v_of(s, x)
+    value = v * (1.0 - SHIFTS[degree])
+    value = value + c_ref[cz_at(s, x)] * (v - next_z(v, v_side[half], place))
+    value = value + c_ref[back_at(s, x)] * (v - previous_z(v, v_side[half], place))
+    for t in range(SPECIES):
+        value = value + main_ref[r_at(s, t, x)] * v_of(t, x)
+    if after:
+        value = value + c_ref[cx_at(s, x)] * (v - v_of(s, x + 1))
+    if before:
+        value = value + c_ref[cx_at(s, x - 1)] * (v - v_of(s, x - 1))
+    along = c_ref[cy_at(s, x)] * (v - next_y(v))
+    return value + (along - roll(along, 1, 0))
+
+
 def step(degree, planes, v_of, v_side, main_ref, side_ref, c_ref, c_side, mask, store, sides=True):
-    lane = iota((ROWS, 128), 1)
     for x in planes:
         factor = DAMPING * mask_of(x, mask[0], *mask[2:])
-        here = [v_of(t, x) for t in range(SPECIES)]
         for s in range(SPECIES):
-            half, place, v = s // 2, slot_of(s, x), here[s]
-            value = v * (1.0 - SHIFTS[degree])
-            value = value + c_ref[cz_at(s, x)] * (v - next_z(v, v_side[half], place))
-            value = value + c_ref[back_at(s, x)] * (v - previous_z(v, v_side[half], place))
-            for t in range(SPECIES):
-                value = value + main_ref[r_at(s, t, x)] * here[t]
-            value = value + c_ref[cx_at(s, x)] * (v - v_of(s, x + 1))
-            value = value + c_ref[cx_at(s, x - 1)] * (v - v_of(s, x - 1))
-            along = c_ref[cy_at(s, x)] * (v - next_y(v))
-            value = value + (along - roll(along, 1, 0))
-            store(s, x, value * factor)
+            store(s, x, plane_sum(degree, s, x, v_of, v_side, main_ref, c_ref) * factor)
     if not sides:
         return None
     return side_step(degree, columns(planes, v_of), v_side, side_ref, c_side, mask)
@@ -450,8 +473,8 @@
     out_ref[8 * s + 2 * x + 1] = value[8:16]
 
 
-def first_steps(r_ref, x_before, x_after, edge_ref, v_in, d_in, c_early, sum_ref, d_edge, v_edge, own_before, own_after, more_before, more_after, v1_ref, v2_ref, wide_ref, wide_side, low_ref, high_ref, side_ref, z_ref, c_side, v_mid):
-    main_ref = Planes(own_planes(None, None, r_ref, x_before, x_after), edge_ref)
+def first_steps(r_ref, x_before, x_after, edge_own, edge_more, v_in, d_in, c_early, sum_ref, d_edge, v_edge, own_before, own_after, more_before, more_after, v1_ref, v2_ref, wide_ref, wide_side, low_ref, high_ref, side_ref, z_ref, c_side, v_mid):
+    main_ref = Planes(own_planes(None, None, r_ref, x_before, x_after), edge_own, edge_more)
     lane = iota((ROWS, 128), 1)
     for side in range(SIDES):
         side_ref[side] = unpack_z(side, own_before, own_after, more_before, more_after)
@@ -492,8 +515,22 @@
             face[FACE_SIDE + n] = packed[8 * n : 8 * n + 8]
 
 
-def last_steps(r_ref, x_before, x_after, edge_ref, side_ref, c_early, z_ref, c_side, wide_ref, wide_side, before_ref, after_ref, q_ref, v1_ref, v2_ref, sums_in, v3_ref, v4_ref, sums_ref, v_in, v_mid):
-    main_ref = Planes(own_planes(None, None, r_ref, x_before, x_after), edge_ref)
+def middle_step(r_ref, x_before, x_after, edge_own, edge_more, c_early, z_ref, wide_ref, wide_side, sum_ref, v_edge):
+    main_ref = Planes(own_planes(None, None, r_ref, x_before, x_after), edge_own, edge_more)
+    c_ref = Conducts(c_early, z_ref)
+
+    def v_of(s, x):
+        return wide_ref[4 * s + x]
+
+    for x in range(4):
+        for s in range(SPECIES):
+            sum_ref[4 * s + x] = plane_sum(2, s, x, v_of, wide_side, main_ref, c_ref, x > 0, x < 3)
+    for half, value in enumerate(columns(range(4), v_of)):
+        v_edge[half] = value
+
+
+def last_steps(r_ref, x_before, x_after, edge_own, edge_more, side_ref, c_early, z_ref, c_side, wide_ref, wide_side, sum_ref, v_edge, before_ref, after_ref, q_ref, v1_ref, v2_ref, sums_in, v3_ref, v4_ref, sums_ref, v_in, v_mid):
+    main_ref = Planes(own_planes(None, None, r_ref, x_before, x_after), edge_own, edge_more)
     c_ref = Conducts(c_early, z_ref)
     mask = masks()
     for s in range(SPECIES):
@@ -524,7 +561,20 @@
         put_own(v4_ref, s, x, value)
 
     more = (main_ref, side_ref, c_ref, c_side, mask)
-    v_side = step(2, R_PLANES, first, v_side, *more, store_mid)
+    for x in R_PLANES:
+        factor = DAMPING * mask_of(x, mask[0], *mask[2:])
+        for s in range(SPECIES):
+            if 0 <= x < 4:
+                value = sum_ref[4 * s + x]
+                if x == 0:
+                    value = value + c_ref[cx_at(s, -1)] * (first(s, 0) - first(s, -1))
+                if x == 3:
+                    value = value + c_ref[cx_at(s, 3)] * (first(s, 3) - first(s, 4))
+            else:
+                value = plane_sum(2, s, x, first, v_side, main_ref, c_ref)
+            store_mid(s, x, value * factor)
+    edges = [v_edge[half] + more for half, more in enumerate(columns((-1, 4), first))]
+    v_side = side_step(2, edges, v_side, side_ref, c_side, mask)
     step(3, range(4), lambda s, x: v_mid[v_at(s, x)], v_side, *more, store_last, sides=False)
 
     def load(i):
@@ -684,7 +734,10 @@
     faces = call(more_y_faces, [face, face], 1 << 20, *x_halos)
     y_more = exchange("gy", *faces)
     face = (2 * BLOCKS, 8, span_z)
-    edge, low, high = call(more_z_faces, [(PLANES, 8, span_z), face, face], 1 << 20, *x_halos, *y_own, *y_more)
+    edges = (PLANES, 8, span_z)
+    edge_own, low, high = call(some_z_faces, [edges, face, face], 1 << 20, *x_halos, *y_own)
+    edge_more, low, high = call(more_z_faces, [edges, face, face], 1 << 20, *y_more, low, high)
+    edge = (edge_own, edge_more)
     z_more = exchange("gz", low, high)
     basis = earlier_basis.reshape(EARLIER, tiles, 8, span_z)
     (sums,) = call(earlier_products, [(8, span_z)], 4 << 20, basis)
@@ -696,7 +749,7 @@
         1 << 20,
         *kept,
         *x_halos,
-        edge,
+        *edge,
     )
     scratch = [pltpu.VMEM((D_BASE,) + plane, jnp.float32)]
     face = (FACE_TILES, 8, span_z)
@@ -708,7 +761,7 @@
         1 << 20,
         reaction,
         *x_halos,
-        edge,
+        *edge,
         *early,
         *z_own,
         *z_more,
@@ -716,19 +769,32 @@
     )
     halos = exchange("gx", low, high)
     (sums,) = call(middle_products, [(8, span_z)], 4 << 20, basis, v1, v2, sums)
+    plane_sums = call(
+        middle_step,
+        [(SPECIES * span_x,) + plane, (HALVES,) + plane],
+        1 << 20,
+        reaction,
+        *x_halos,
+        *edge,
+        early[2],
+        z_conducts,
+        wide,
+        wide_side,
+    )
     v3, v4, rows = call(
         last_steps,
         [own, own, (devices, span_z)],
         1 << 20,
         reaction,
         *x_halos,
-        edge,
+        *edge,
         side,
         early[2],
         z_conducts,
         side_conducts,
         wide,
         wide_side,
+        *plane_sums,
         *halos,
         basis,
         v1,

time: 64.1 us -> 63.3 us (0.988)
  waiting for transfers between devices: 6.75 us -> 5.85 us
    ppermute x10, waiting for transfers between devices: 6.19 us -> 5.3 us  [exchange(): return (lax.ppermute(high, axis, up), lax.ppermute(low, axis, down))]
    pallas_call x10 -> x12, Pallas kernels: 8.89 us -> 8.95 us  [call(): pl.pallas_call(body, out_shape=[jax.ShapeDtypeStruct(shape, jnp.float32)...]
  transfers between devices with their start and end apart: 12 -> 12, of which waited for: 6 -> 6; matrix products, arithmetic and copies ran while one was open for 0% -> 0% of each run, Pallas kernels for 4% -> 5%
where the time goes in v2:
time: 63.3 us; the launch traced here: 63.1 us
  blocking collectives  26.5 us (42%)
  starting transfers between devices  21.1 us (33%)
  Pallas kernels  8.95 us (14%)
  waiting for transfers between devices  5.85 us (9%)
  between operations  0.73 us (1%)
    all_to_all x1, blocking collectives, on_device(): rows = lax.all_to_all(rows.reshape(devices, 1, span_z), AXES, 0, 0)  26.5 us
    ppermute x10, starting transfers between devices, exchange(): return (lax.ppermute(high, axis, up), lax.ppermute(low, axis, down))  18.5 us
    pallas_call x12, Pallas kernels, call(): pl.pallas_call(body, out_shape=[jax.ShapeDtypeStruct(shape, jnp.float32)...  8.95 us
    ppermute x10, waiting for transfers between devices, exchange(): return (lax.ppermute(high, axis, up), lax.ppermute(low, axis, down))  5.3 us
    ppermute x1, starting transfers between devices, on_device(): z_after = lax.ppermute(own[2], 'gz', down)  2.67 us
  transfers between devices with their start and end apart: 12, of which 6 were waited for; matrix products, arithmetic and copies ran while one was open for 0% of the time, Pallas kernels for 5%

profile of v2, /device:TPU:1, one launch (start us, length us, event | category | flops | bytes accessed | tf_op | source)
XLA Modules:
  0.0 63.1 jit_solution(11685497106727028363)
XLA Ops:
  0.6 1.3 %shard_map.58 = (f32[32,16,128]{2,1,0:T(8,128)S(1)}, f32[32,16,128]{2,1,0:T(8,128)S(1)}, f32[4,4,16,128]{3,2,1,0:T(8,128)S(1)}, f32[4,4,16,128]{3,2,1,0:T(8,128)S(1)}) custom-call(f32[8,4,4,16,128]{4,3,2,1,0:T(8,128)} %q_ref.1, f32[4,4,16,128]{3,2,1,0:T(8,128)} %d_ref.1, f32[4,4,4,16,128]{4,3,2,1,0:T(8,128)} %r_ref.11), custom_call_target="tpu_custom_call" | custom-call | flops 1048576 | bytes 1048576 | tf_op jit(solution)/shard_map/pallas_call | solution.py:684
  2.0 2.1 %collective-permute-start = (f32[32,16,128]{2,1,0:T(8,128)S(1)}, f32[32,16,128]{2,1,0:T(8,128)S(1)}, u32[]{:S(2)}, u32[]{:S(2)}) collective-permute-start(f32[32,16,128]{2,1,0:T(8,128)S(1)} %get-tuple-element.42), channel_id=1, source_target_pairs={{0,64},{64,128},{128,192},{192,0},{1,65},{65,129},{129,193},{193,1... | collective-permute-start | bytes 786440 | tf_op jit(solution)/shard_map/ppermute | solution.py:701
  4.1 1.4 %collective-permute-start.1 = (f32[32,16,128]{2,1,0:T(8,128)S(1)}, f32[32,16,128]{2,1,0:T(8,128)S(1)}, u32[]{:S(2)}, u32[]{:S(2)}) collective-permute-start(f32[32,16,128]{2,1,0:T(8,128)S(1)} %get-tuple-element.43), channel_id=1, source_target_pairs={{64,0},{128,64},{192,128},{0,192},{65,1},{129,65},{193,129},{1,193... | collective-permute-start | bytes 786440 | tf_op jit(solution)/shard_map/ppermute | solution.py:701
  5.4 0.5 shard_map.59
  5.9 2.5 %collective-permute-start.2 = (f32[48,8,128]{2,1,0:T(8,128)S(1)}, f32[48,8,128]{2,1,0:T(8,128)S(1)}, u32[]{:S(2)}, u32[]{:S(2)}) collective-permute-start(f32[48,8,128]{2,1,0:T(8,128)S(1)} %get-tuple-element.46), channel_id=1, source_target_pairs={{0,8},{8,16},{16,24},{24,32},{32,40},{40,48},{48,56},{56,0},{1,9},... | collective-permute-start | bytes 589832 | tf_op jit(solution)/shard_map/ppermute | solution.py:701
  8.5 0.6 collective-permute-start.3
  9.1 1.6 %collective-permute-done.1.x_after.after_ref = f32[32,16,128]{2,1,0:T(8,128)S(1)} collective-permute-done((f32[32,16,128]{2,1,0:T(8,128)S(1)}, f32[32,16,128]{2,1,0:T(8,128)S(1)}, u32[]{:S(2)}, u32[]{:S(2)}) %collective-permute-start.1) | collective-permute-done | bytes 262176 | tf_op jit(solution)/shard_map/ppermute | solution.py:701
  10.7 3.3 %collective-permute-start.4 = (f32[20,8,128]{2,1,0:T(8,128)S(1)}, f32[20,8,128]{2,1,0:T(8,128)S(1)}, u32[]{:S(2)}, u32[]{:S(2)}) collective-permute-start(f32[20,8,128]{2,1,0:T(8,128)S(1)} %get-tuple-element.49), channel_id=1, source_target_pairs={{0,8},{8,16},{16,24},{24,32},{32,40},{40,48},{48,56},{56,0},{1,9},... | collective-permute-start | bytes 245768 | tf_op jit(solution)/shard_map/ppermute | solution.py:701
  14.1 0.5 shard_map.60
  14.6 0.9 %collective-permute-done.4.y_before = f32[20,8,128]{2,1,0:T(8,128)S(1)} collective-permute-done((f32[20,8,128]{2,1,0:T(8,128)S(1)}, f32[20,8,128]{2,1,0:T(8,128)S(1)}, u32[]{:S(2)}, u32[]{:S(2)}) %collective-permute-start.4) | collective-permute-done | bytes 81952 | tf_op jit(solution)/shard_map/ppermute | solution.py:701
  15.5 2.4 %collective-permute-done.5.y_after = f32[20,8,128]{2,1,0:T(8,128)S(1)} collective-permute-done((f32[20,8,128]{2,1,0:T(8,128)S(1)}, f32[20,8,128]{2,1,0:T(8,128)S(1)}, u32[]{:S(2)}, u32[]{:S(2)}) %collective-permute-start.5) | collective-permute-done | bytes 81952 | tf_op jit(solution)/shard_map/ppermute | solution.py:701
  18.1 1.7 %collective-permute-start.8 = (f32[12,8,128]{2,1,0:T(8,128)S(1)}, f32[12,8,128]{2,1,0:T(8,128)S(1)}, u32[]{:S(2)}, u32[]{:S(2)}) collective-permute-start(f32[12,8,128]{2,1,0:T(8,128)S(1)} %get-tuple-element.62), channel_id=1, source_target_pairs={{0,1},{1,2},{2,3},{3,4},{4,5},{5,6},{6,7},{7,0},{8,9},{9,10},{10,1... | collective-permute-start | bytes 147464 | tf_op jit(solution)/shard_map/ppermute | solution.py:701
  19.8 4.0 %collective-permute-start.9 = (f32[12,8,128]{2,1,0:T(8,128)S(1)}, f32[12,8,128]{2,1,0:T(8,128)S(1)}, u32[]{:S(2)}, u32[]{:S(2)}) collective-permute-start(f32[12,8,128]{2,1,0:T(8,128)S(1)} %get-tuple-element.63), channel_id=1, source_target_pairs={{1,0},{2,1},{3,2},{4,3},{5,4},{6,5},{7,6},{0,7},{9,8},{10,9},{11,1... | collective-permute-start | bytes 147464 | tf_op jit(solution)/shard_map/ppermute | solution.py:701
  23.9 2.7 %collective-permute-start.7 = (f32[3,16,128]{2,1,0:T(8,128)S(1)}, f32[3,16,128]{2,1,0:T(8,128)S(1)}, u32[]{:S(2)}, u32[]{:S(2)}) collective-permute-start(f32[3,16,128]{2,1,0:T(8,128)S(1)} %get-tuple-element.61), channel_id=1, source_target_pairs={{1,0},{2,1},{3,2},{4,3},{5,4},{6,5},{7,6},{0,7},{9,8},{10,9},{11,1... | collective-permute-start | bytes 73736 | tf_op jit(solution)/shard_map/ppermute | solution.py:731
  26.5 0.7 %shard_map.63 = (f32[32,24,128]{2,1,0:T(8,128)S(1)}, f32[32,24,128]{2,1,0:T(8,128)S(1)}, f32[100,24,128]{2,1,0:T(8,128)S(1)}, f32[24,24,128]{2,1,0:T(8,128)S(1)}...) custom-call(f32[4,4,16,128]{3,2,1,0:T(8,128)S(1)} %get-tuple-element.44.v_ref, ...), custom_call_target="tpu_custom_call" | custom-call | flops 1048576 | bytes 1048576 | tf_op jit(solution)/shard_map/pallas_call | solution.py:684
  27.2 0.5 collective-permute-done.6.own_before
  27.8 1.1 %shard_map.64 = (f32[32,8,128]{2,1,0:T(8,128)S(1)}, f32[32,8,128]{2,1,0:T(8,128)S(1)}, f32[16,24,128]{2,1,0:T(8,128)S(1)}, f32[2,24,128]{2,1,0:T(8,128)S(1)}, f3...) custom-call(f32[4,4,4,16,128]{4,3,2,1,0:T(8,128)S(1)} %copy-done.1, ...), custom_call_target="tpu_custom_call" | custom-call | flops 1048576 | bytes 1048576 | tf_op jit(solution)/shard_map/pallas_call | solution.py:684
  28.9 1.3 %collective-permute-start.10 = (f32[23,8,128]{2,1,0:T(8,128)S(1)}, f32[23,8,128]{2,1,0:T(8,128)S(1)}, u32[]{:S(2)}, u32[]{:S(2)}) collective-permute-start(f32[23,8,128]{2,1,0:T(8,128)S(1)} %get-tuple-element.71), channel_id=1, source_target_pairs={{0,64},{64,128},{128,192},{192,0},{1,65},{65,129},{129,193},{193,1... | collective-permute-start | bytes 282632 | tf_op jit(solution)/shard_map/ppermute | solution.py:701
  30.2 1.6 %collective-permute-start.11 = (f32[23,8,128]{2,1,0:T(8,128)S(1)}, f32[23,8,128]{2,1,0:T(8,128)S(1)}, u32[]{:S(2)}, u32[]{:S(2)}) collective-permute-start(f32[23,8,128]{2,1,0:T(8,128)S(1)} %get-tuple-element.72), channel_id=1, source_target_pairs={{64,0},{128,64},{192,128},{0,192},{65,1},{129,65},{193,129},{1,193... | collective-permute-start | bytes 282632 | tf_op jit(solution)/shard_map/ppermute | solution.py:701
  31.7 0.7 %shard_map.66.before_ref = f32[8,128]{1,0:T(8,128)S(1)} custom-call(f32[8,32,8,128]{3,2,1,0:T(8,128)S(1)} %bitcast.7), custom_call_target="tpu_custom_call" | custom-call | flops 4194304 | bytes 4194304 | tf_op jit(solution)/shard_map/pallas_call | solution.py:684
  32.8 0.5 shard_map.67.sums_in
  33.6 1.1 %shard_map.68 = (f32[32,8,128]{2,1,0:T(8,128)S(1)}, f32[32,8,128]{2,1,0:T(8,128)S(1)}, f32[256,128]{1,0:T(8,128)S(1)}) custom-call(f32[4,4,4,16,128]{4,3,2,1,0:T(8,128)S(1)} %copy-done.1, f32[32,16,128]{2,1,0:T(8,128)S(1)} %collective-permute-done.x_before.before_ref, f32[32,16,128]{2,1,0:T(8,128)S(1)} %collective-permute-done.1.x_after.after_ref, ...), custom_call_target="tpu_custom_call" | custom-call | flops 1048576 | bytes 1048576 | tf_op jit(solution)/shard_map/pallas_call | solution.py:684
  34.7 26.5 %all_to_all.5 = f32[256,1,128]{2,1,0:T(1,128)S(1)} all-to-all(f32[256,1,128]{2,1,0:T(1,128)S(1)} %bitcast.12), channel_id=1, replica_groups=mesh['gx'=4,'gy'=8,'gz'=8] {'gx','gy','gz'}, dimensions={0} | all-to-all | bytes 262144 | tf_op jit(solution)/shard_map/all_to_all | solution.py:805
  61.2 1.9 %shard_map.69 = (f32[4,32,8,128]{3,2,1,0:T(8,128)}, f32[4,8]{1,0:T(4,128)}, f32[4,4]{1,0:T(4,128)}) custom-call(f32[32,8,128]{2,1,0:T(8,128)S(1)} %bitcast.11, f32[8,32,8,128]{3,2,1,0:T(8,128)S(1)} %bitcast.10, f32[32,8,128]{2,1,0:T(8,128)S(1)} %get-tuple-element.73.v1_ref.refs_0_, f32[32,8,128]{2,1,0:T(8,128)S(1)} %get-tuple-element.74.v2_ref.refs_1_, ...), custom_call_target="tpu_custom_call" | custom-call | flops 1048576 | bytes 1048576 | tf_op jit(solution)/shard_map/pallas_call | solution.py:684
  (17 shorter events, 1.0 us)
Async XLA Ops:
  0.6 4.8 %copy-start.1 = (f32[4,4,4,16,128]{4,3,2,1,0:T(8,128)S(1)}, f32[4,4,4,16,128]{4,3,2,1,0:T(8,128)}, u32[]{:S(2)}) copy-start(f32[4,4,4,16,128]{4,3,2,1,0:T(8,128)} %r_ref.11) | copy-start | bytes 1572868
  2.0 7.1 %collective-permute-start = (f32[32,16,128]{2,1,0:T(8,128)S(1)}, f32[32,16,128]{2,1,0:T(8,128)S(1)}, u32[]{:S(2)}, u32[]{:S(2)}) collective-permute-start(f32[32,16,128]{2,1,0:T(8,128)S(1)} %get-tuple-element.42), channel_id=1, source_target_pairs={{0,64},{64,128},{128,192},{192,0},{1,65},{65,129},{129,193},{193,1... | collective-permute-start | bytes 786440 | tf_op jit(solution)/shard_map/ppermute | solution.py:701
  4.1 6.6 %collective-permute-start.1 = (f32[32,16,128]{2,1,0:T(8,128)S(1)}, f32[32,16,128]{2,1,0:T(8,128)S(1)}, u32[]{:S(2)}, u32[]{:S(2)}) collective-permute-start(f32[32,16,128]{2,1,0:T(8,128)S(1)} %get-tuple-element.43), channel_id=1, source_target_pairs={{64,0},{128,64},{192,128},{0,192},{65,1},{129,65},{193,129},{1,193... | collective-permute-start | bytes 786440 | tf_op jit(solution)/shard_map/ppermute | solution.py:701
  5.9 8.1 %collective-permute-start.2 = (f32[48,8,128]{2,1,0:T(8,128)S(1)}, f32[48,8,128]{2,1,0:T(8,128)S(1)}, u32[]{:S(2)}, u32[]{:S(2)}) collective-permute-start(f32[48,8,128]{2,1,0:T(8,128)S(1)} %get-tuple-element.46), channel_id=1, source_target_pairs={{0,8},{8,16},{16,24},{24,32},{32,40},{40,48},{48,56},{56,0},{1,9},... | collective-permute-start | bytes 589832 | tf_op jit(solution)/shard_map/ppermute | solution.py:701
  8.5 5.6 %collective-permute-start.3 = (f32[48,8,128]{2,1,0:T(8,128)S(1)}, f32[48,8,128]{2,1,0:T(8,128)S(1)}, u32[]{:S(2)}, u32[]{:S(2)}) collective-permute-start(f32[48,8,128]{2,1,0:T(8,128)S(1)} %get-tuple-element.47), channel_id=1, source_target_pairs={{8,0},{16,8},{24,16},{32,24},{40,32},{48,40},{56,48},{0,56},{9,1},... | collective-permute-start | bytes 589832 | tf_op jit(solution)/shard_map/ppermute | solution.py:701
  10.7 4.8 %collective-permute-start.4 = (f32[20,8,128]{2,1,0:T(8,128)S(1)}, f32[20,8,128]{2,1,0:T(8,128)S(1)}, u32[]{:S(2)}, u32[]{:S(2)}) collective-permute-start(f32[20,8,128]{2,1,0:T(8,128)S(1)} %get-tuple-element.49), channel_id=1, source_target_pairs={{0,8},{8,16},{16,24},{24,32},{32,40},{40,48},{48,56},{56,0},{1,9},... | collective-permute-start | bytes 245768 | tf_op jit(solution)/shard_map/ppermute | solution.py:701
  14.0 3.9 %collective-permute-start.5 = (f32[20,8,128]{2,1,0:T(8,128)S(1)}, f32[20,8,128]{2,1,0:T(8,128)S(1)}, u32[]{:S(2)}, u32[]{:S(2)}) collective-permute-start(f32[20,8,128]{2,1,0:T(8,128)S(1)} %get-tuple-element.50), channel_id=1, source_target_pairs={{8,0},{16,8},{24,16},{32,24},{40,32},{48,40},{56,48},{0,56},{9,1},... | collective-permute-start | bytes 245768 | tf_op jit(solution)/shard_map/ppermute | solution.py:701
  18.1 9.6 %collective-permute-start.8 = (f32[12,8,128]{2,1,0:T(8,128)S(1)}, f32[12,8,128]{2,1,0:T(8,128)S(1)}, u32[]{:S(2)}, u32[]{:S(2)}) collective-permute-start(f32[12,8,128]{2,1,0:T(8,128)S(1)} %get-tuple-element.62), channel_id=1, source_target_pairs={{0,1},{1,2},{2,3},{3,4},{4,5},{5,6},{6,7},{7,0},{8,9},{9,10},{10,1... | collective-permute-start | bytes 147464 | tf_op jit(solution)/shard_map/ppermute | solution.py:701
  19.8 7.9 %collective-permute-start.9 = (f32[12,8,128]{2,1,0:T(8,128)S(1)}, f32[12,8,128]{2,1,0:T(8,128)S(1)}, u32[]{:S(2)}, u32[]{:S(2)}) collective-permute-start(f32[12,8,128]{2,1,0:T(8,128)S(1)} %get-tuple-element.63), channel_id=1, source_target_pairs={{1,0},{2,1},{3,2},{4,3},{5,4},{6,5},{7,6},{0,7},{9,8},{10,9},{11,1... | collective-permute-start | bytes 147464 | tf_op jit(solution)/shard_map/ppermute | solution.py:701
  23.9 3.9 %collective-permute-start.6 = (f32[3,16,128]{2,1,0:T(8,128)S(1)}, f32[3,16,128]{2,1,0:T(8,128)S(1)}, u32[]{:S(2)}, u32[]{:S(2)}) collective-permute-start(f32[3,16,128]{2,1,0:T(8,128)S(1)} %get-tuple-element.60), channel_id=1, source_target_pairs={{0,1},{1,2},{2,3},{3,4},{4,5},{5,6},{6,7},{7,0},{8,9},{9,10},{10,1... | collective-permute-start | bytes 73736 | tf_op jit(solution)/shard_map/ppermute | solution.py:730
  23.9 3.9 %collective-permute-start.7 = (f32[3,16,128]{2,1,0:T(8,128)S(1)}, f32[3,16,128]{2,1,0:T(8,128)S(1)}, u32[]{:S(2)}, u32[]{:S(2)}) collective-permute-start(f32[3,16,128]{2,1,0:T(8,128)S(1)} %get-tuple-element.61), channel_id=1, source_target_pairs={{1,0},{2,1},{3,2},{4,3},{5,4},{6,5},{7,6},{0,7},{9,8},{10,9},{11,1... | collective-permute-start | bytes 73736 | tf_op jit(solution)/shard_map/ppermute | solution.py:731
  27.8 4.0 %copy-start = (f32[8,4,4,16,128]{4,3,2,1,0:T(8,128)S(1)}, f32[8,4,4,16,128]{4,3,2,1,0:T(8,128)}, u32[]{:S(2)}) copy-start(f32[8,4,4,16,128]{4,3,2,1,0:T(8,128)} %q_ref.1) | copy-start | bytes 3145732
  28.9 4.7 %collective-permute-start.10 = (f32[23,8,128]{2,1,0:T(8,128)S(1)}, f32[23,8,128]{2,1,0:T(8,128)S(1)}, u32[]{:S(2)}, u32[]{:S(2)}) collective-permute-start(f32[23,8,128]{2,1,0:T(8,128)S(1)} %get-tuple-element.71), channel_id=1, source_target_pairs={{0,64},{64,128},{128,192},{192,0},{1,65},{65,129},{129,193},{193,1... | collective-permute-start | bytes 282632 | tf_op jit(solution)/shard_map/ppermute | solution.py:701
  30.2 3.4 %collective-permute-start.11 = (f32[23,8,128]{2,1,0:T(8,128)S(1)}, f32[23,8,128]{2,1,0:T(8,128)S(1)}, u32[]{:S(2)}, u32[]{:S(2)}) collective-permute-start(f32[23,8,128]{2,1,0:T(8,128)S(1)} %get-tuple-element.72), channel_id=1, source_target_pairs={{64,0},{128,64},{192,128},{0,192},{65,1},{129,65},{193,129},{1,193... | collective-permute-start | bytes 282632 | tf_op jit(solution)/shard_map/ppermute | solution.py:701

commit v3 on v2

--- a/solution.py
+++ b/solution.py
@@ -597,7 +597,7 @@
         return tuple(total + values[a] * values[b] for total, (a, b) in zip(sums, pairs))
 
     zero = jnp.zeros((8, 128), jnp.float32)
-    sums = lax.fori_loop(0, count, body, (zero,) * len(pairs))
+    sums = lax.fori_loop(0, count, body, (zero,) * len(pairs), unroll=4)
     lane = lax.broadcasted_iota(jnp.int32, (8, 128), 1)
     row = zero
     for total, pair in zip(sums, pairs):
@@ -616,9 +616,10 @@
 
 def finish_kernel(entries, sums_ref, q_ref, *refs):
     v_refs, (new_ref, coeff_ref, triangle_ref) = refs[:STEPS], refs[STEPS:]
-    total = sums_ref[0]
-    for i in range(1, sums_ref.shape[0]):
-        total = total + sums_ref[i]
+    parts = [sums_ref[i] for i in range(sums_ref.shape[0])]
+    while len(parts) > 1:
+        parts = [parts[i] + parts[i + 1] for i in range(0, len(parts), 2)]
+    total = parts[0]
     total = jnp.broadcast_to(jnp.sum(total, 0, keepdims=True), total.shape) * (1.0 / entries)
 
     def entry(a, b):
@@ -645,8 +646,8 @@
         pivot = gram[(k, k)]
         for m in range(k):
             pivot = pivot - factor[(k, m)] * factor[(k, m)]
-        factor[(k, k)] = jnp.sqrt(pivot)
-        inverse.append(1.0 / factor[(k, k)])
+        inverse.append(lax.rsqrt(pivot))
+        factor[(k, k)] = pivot * inverse[k]
         for j in range(k + 1, STEPS):
             value = gram[(j, k)]
             for m in range(k):
@@ -677,7 +678,7 @@
             new_ref[j, n] = done[j]
         return carry
 
-    lax.fori_loop(0, q_ref.shape[1], body, 0)
+    lax.fori_loop(0, q_ref.shape[1], body, 0, unroll=8)
 
 
 def call(body, outs, cost, *args, **more):

time: 63.3 us -> 62.6 us (0.989)
  Pallas kernels: 8.95 us -> 7.9 us
    pallas_call x12, Pallas kernels: 8.95 us -> 7.9 us  [call(): pl.pallas_call(body, out_shape=[jax.ShapeDtypeStruct(shape, jnp.float32)...]
where the time goes in v3:
time: 62.6 us; the launch traced here: 62.5 us
  blocking collectives  26.5 us (42%)
  starting transfers between devices  21.1 us (34%)
  Pallas kernels  7.9 us (13%)
  waiting for transfers between devices  6.26 us (10%)
  between operations  0.73 us (1%)
    all_to_all x1, blocking collectives, on_device(): rows = lax.all_to_all(rows.reshape(devices, 1, span_z), AXES, 0, 0)  26.5 us
    ppermute x10, starting transfers between devices, exchange(): return (lax.ppermute(high, axis, up), lax.ppermute(low, axis, down))  18.5 us
    pallas_call x12, Pallas kernels, call(): pl.pallas_call(body, out_shape=[jax.ShapeDtypeStruct(shape, jnp.float32)...  7.9 us
    ppermute x10, waiting for transfers between devices, exchange(): return (lax.ppermute(high, axis, up), lax.ppermute(low, axis, down))  5.71 us
    ppermute x1, starting transfers between devices, on_device(): z_after = lax.ppermute(own[2], 'gz', down)  2.67 us
  transfers between devices with their start and end apart: 12, of which 6 were waited for; matrix products, arithmetic and copies ran while one was open for 0% of the time, Pallas kernels for 5%

profile of v3, /device:TPU:1, one launch (start us, length us, event | category | flops | bytes accessed | tf_op | source)
XLA Modules:
  0.0 62.5 jit_solution(11400018148628718107)
XLA Ops:
  0.6 1.3 %shard_map.58 = (f32[32,16,128]{2,1,0:T(8,128)S(1)}, f32[32,16,128]{2,1,0:T(8,128)S(1)}, f32[4,4,16,128]{3,2,1,0:T(8,128)S(1)}, f32[4,4,16,128]{3,2,1,0:T(8,128)S(1)}) custom-call(f32[8,4,4,16,128]{4,3,2,1,0:T(8,128)} %q_ref.1, f32[4,4,16,128]{3,2,1,0:T(8,128)} %d_ref.1, f32[4,4,4,16,128]{4,3,2,1,0:T(8,128)} %r_ref.11), custom_call_target="tpu_custom_call" | custom-call | flops 1048576 | bytes 1048576 | tf_op jit(solution)/shard_map/pallas_call | solution.py:685
  2.0 2.1 %collective-permute-start = (f32[32,16,128]{2,1,0:T(8,128)S(1)}, f32[32,16,128]{2,1,0:T(8,128)S(1)}, u32[]{:S(2)}, u32[]{:S(2)}) collective-permute-start(f32[32,16,128]{2,1,0:T(8,128)S(1)} %get-tuple-element.42), channel_id=1, source_target_pairs={{0,64},{64,128},{128,192},{192,0},{1,65},{65,129},{129,193},{193,1... | collective-permute-start | bytes 786440 | tf_op jit(solution)/shard_map/ppermute | solution.py:702
  4.1 1.4 %collective-permute-start.1 = (f32[32,16,128]{2,1,0:T(8,128)S(1)}, f32[32,16,128]{2,1,0:T(8,128)S(1)}, u32[]{:S(2)}, u32[]{:S(2)}) collective-permute-start(f32[32,16,128]{2,1,0:T(8,128)S(1)} %get-tuple-element.43), channel_id=1, source_target_pairs={{64,0},{128,64},{192,128},{0,192},{65,1},{129,65},{193,129},{1,193... | collective-permute-start | bytes 786440 | tf_op jit(solution)/shard_map/ppermute | solution.py:702
  5.4 0.5 shard_map.59
  5.9 2.5 %collective-permute-start.2 = (f32[48,8,128]{2,1,0:T(8,128)S(1)}, f32[48,8,128]{2,1,0:T(8,128)S(1)}, u32[]{:S(2)}, u32[]{:S(2)}) collective-permute-start(f32[48,8,128]{2,1,0:T(8,128)S(1)} %get-tuple-element.46), channel_id=1, source_target_pairs={{0,8},{8,16},{16,24},{24,32},{32,40},{40,48},{48,56},{56,0},{1,9},... | collective-permute-start | bytes 589832 | tf_op jit(solution)/shard_map/ppermute | solution.py:702
  8.5 0.6 collective-permute-start.3
  9.1 1.6 %collective-permute-done.1.x_after.after_ref = f32[32,16,128]{2,1,0:T(8,128)S(1)} collective-permute-done((f32[32,16,128]{2,1,0:T(8,128)S(1)}, f32[32,16,128]{2,1,0:T(8,128)S(1)}, u32[]{:S(2)}, u32[]{:S(2)}) %collective-permute-start.1) | collective-permute-done | bytes 262176 | tf_op jit(solution)/shard_map/ppermute | solution.py:702
  10.7 3.3 %collective-permute-start.4 = (f32[20,8,128]{2,1,0:T(8,128)S(1)}, f32[20,8,128]{2,1,0:T(8,128)S(1)}, u32[]{:S(2)}, u32[]{:S(2)}) collective-permute-start(f32[20,8,128]{2,1,0:T(8,128)S(1)} %get-tuple-element.49), channel_id=1, source_target_pairs={{0,8},{8,16},{16,24},{24,32},{32,40},{40,48},{48,56},{56,0},{1,9},... | collective-permute-start | bytes 245768 | tf_op jit(solution)/shard_map/ppermute | solution.py:702
  14.1 0.5 shard_map.60
  14.6 0.9 %collective-permute-done.4.y_before = f32[20,8,128]{2,1,0:T(8,128)S(1)} collective-permute-done((f32[20,8,128]{2,1,0:T(8,128)S(1)}, f32[20,8,128]{2,1,0:T(8,128)S(1)}, u32[]{:S(2)}, u32[]{:S(2)}) %collective-permute-start.4) | collective-permute-done | bytes 81952 | tf_op jit(solution)/shard_map/ppermute | solution.py:702
  15.5 2.4 %collective-permute-done.5.y_after = f32[20,8,128]{2,1,0:T(8,128)S(1)} collective-permute-done((f32[20,8,128]{2,1,0:T(8,128)S(1)}, f32[20,8,128]{2,1,0:T(8,128)S(1)}, u32[]{:S(2)}, u32[]{:S(2)}) %collective-permute-start.5) | collective-permute-done | bytes 81952 | tf_op jit(solution)/shard_map/ppermute | solution.py:702
  18.1 1.7 %collective-permute-start.8 = (f32[12,8,128]{2,1,0:T(8,128)S(1)}, f32[12,8,128]{2,1,0:T(8,128)S(1)}, u32[]{:S(2)}, u32[]{:S(2)}) collective-permute-start(f32[12,8,128]{2,1,0:T(8,128)S(1)} %get-tuple-element.62), channel_id=1, source_target_pairs={{0,1},{1,2},{2,3},{3,4},{4,5},{5,6},{6,7},{7,0},{8,9},{9,10},{10,1... | collective-permute-start | bytes 147464 | tf_op jit(solution)/shard_map/ppermute | solution.py:702
  19.8 4.0 %collective-permute-start.9 = (f32[12,8,128]{2,1,0:T(8,128)S(1)}, f32[12,8,128]{2,1,0:T(8,128)S(1)}, u32[]{:S(2)}, u32[]{:S(2)}) collective-permute-start(f32[12,8,128]{2,1,0:T(8,128)S(1)} %get-tuple-element.63), channel_id=1, source_target_pairs={{1,0},{2,1},{3,2},{4,3},{5,4},{6,5},{7,6},{0,7},{9,8},{10,9},{11,1... | collective-permute-start | bytes 147464 | tf_op jit(solution)/shard_map/ppermute | solution.py:702
  23.9 2.7 %collective-permute-start.7 = (f32[3,16,128]{2,1,0:T(8,128)S(1)}, f32[3,16,128]{2,1,0:T(8,128)S(1)}, u32[]{:S(2)}, u32[]{:S(2)}) collective-permute-start(f32[3,16,128]{2,1,0:T(8,128)S(1)} %get-tuple-element.61), channel_id=1, source_target_pairs={{1,0},{2,1},{3,2},{4,3},{5,4},{6,5},{7,6},{0,7},{9,8},{10,9},{11,1... | collective-permute-start | bytes 73736 | tf_op jit(solution)/shard_map/ppermute | solution.py:732
  26.5 0.7 %shard_map.63 = (f32[32,24,128]{2,1,0:T(8,128)S(1)}, f32[32,24,128]{2,1,0:T(8,128)S(1)}, f32[100,24,128]{2,1,0:T(8,128)S(1)}, f32[24,24,128]{2,1,0:T(8,128)S(1)}...) custom-call(f32[4,4,16,128]{3,2,1,0:T(8,128)S(1)} %get-tuple-element.44.v_ref, ...), custom_call_target="tpu_custom_call" | custom-call | flops 1048576 | bytes 1048576 | tf_op jit(solution)/shard_map/pallas_call | solution.py:685
  27.2 0.5 collective-permute-done.6.own_before
  27.8 1.1 %shard_map.64 = (f32[32,8,128]{2,1,0:T(8,128)S(1)}, f32[32,8,128]{2,1,0:T(8,128)S(1)}, f32[16,24,128]{2,1,0:T(8,128)S(1)}, f32[2,24,128]{2,1,0:T(8,128)S(1)}, f3...) custom-call(f32[4,4,4,16,128]{4,3,2,1,0:T(8,128)S(1)} %copy-done.1, ...), custom_call_target="tpu_custom_call" | custom-call | flops 1048576 | bytes 1048576 | tf_op jit(solution)/shard_map/pallas_call | solution.py:685
  28.9 1.3 %collective-permute-start.10 = (f32[23,8,128]{2,1,0:T(8,128)S(1)}, f32[23,8,128]{2,1,0:T(8,128)S(1)}, u32[]{:S(2)}, u32[]{:S(2)}) collective-permute-start(f32[23,8,128]{2,1,0:T(8,128)S(1)} %get-tuple-element.71), channel_id=1, source_target_pairs={{0,64},{64,128},{128,192},{192,0},{1,65},{65,129},{129,193},{193,1... | collective-permute-start | bytes 282632 | tf_op jit(solution)/shard_map/ppermute | solution.py:702
  30.2 1.6 %collective-permute-start.11 = (f32[23,8,128]{2,1,0:T(8,128)S(1)}, f32[23,8,128]{2,1,0:T(8,128)S(1)}, u32[]{:S(2)}, u32[]{:S(2)}) collective-permute-start(f32[23,8,128]{2,1,0:T(8,128)S(1)} %get-tuple-element.72), channel_id=1, source_target_pairs={{64,0},{128,64},{192,128},{0,192},{65,1},{129,65},{193,129},{1,193... | collective-permute-start | bytes 282632 | tf_op jit(solution)/shard_map/ppermute | solution.py:702
  31.7 0.5 shard_map.66.before_ref
  32.9 0.7 %collective-permute-done.10.before_ref = f32[23,8,128]{2,1,0:T(8,128)S(1)} collective-permute-done((f32[23,8,128]{2,1,0:T(8,128)S(1)}, f32[23,8,128]{2,1,0:T(8,128)S(1)}, u32[]{:S(2)}, u32[]{:S(2)}) %collective-permute-start.10) | collective-permute-done | bytes 94240 | tf_op jit(solution)/shard_map/ppermute | solution.py:702
  33.6 1.0 %shard_map.68 = (f32[32,8,128]{2,1,0:T(8,128)S(1)}, f32[32,8,128]{2,1,0:T(8,128)S(1)}, f32[256,128]{1,0:T(8,128)S(1)}) custom-call(f32[4,4,4,16,128]{4,3,2,1,0:T(8,128)S(1)} %copy-done.1, f32[32,16,128]{2,1,0:T(8,128)S(1)} %collective-permute-done.x_before.before_ref, f32[32,16,128]{2,1,0:T(8,128)S(1)} %collective-permute-done.1.x_after.after_ref, ...), custom_call_target="tpu_custom_call" | custom-call | flops 1048576 | bytes 1048576 | tf_op jit(solution)/shard_map/pallas_call | solution.py:685
  34.6 26.5 %all_to_all.5 = f32[256,1,128]{2,1,0:T(1,128)S(1)} all-to-all(f32[256,1,128]{2,1,0:T(1,128)S(1)} %bitcast.12), channel_id=1, replica_groups=mesh['gx'=4,'gy'=8,'gz'=8] {'gx','gy','gz'}, dimensions={0} | all-to-all | bytes 262144 | tf_op jit(solution)/shard_map/all_to_all | solution.py:806
  61.0 1.5 %shard_map.69 = (f32[4,32,8,128]{3,2,1,0:T(8,128)}, f32[4,8]{1,0:T(4,128)}, f32[4,4]{1,0:T(4,128)}) custom-call(f32[32,8,128]{2,1,0:T(8,128)S(1)} %bitcast.11, f32[8,32,8,128]{3,2,1,0:T(8,128)S(1)} %bitcast.10, f32[32,8,128]{2,1,0:T(8,128)S(1)} %get-tuple-element.73.v1_ref.refs_0_, f32[32,8,128]{2,1,0:T(8,128)S(1)} %get-tuple-element.74.v2_ref.refs_1_, ...), custom_call_target="tpu_custom_call" | custom-call | flops 1048576 | bytes 1048576 | tf_op jit(solution)/shard_map/pallas_call | solution.py:685
  (17 shorter events, 1.0 us)
Async XLA Ops:
  0.6 4.8 %copy-start.1 = (f32[4,4,4,16,128]{4,3,2,1,0:T(8,128)S(1)}, f32[4,4,4,16,128]{4,3,2,1,0:T(8,128)}, u32[]{:S(2)}) copy-start(f32[4,4,4,16,128]{4,3,2,1,0:T(8,128)} %r_ref.11) | copy-start | bytes 1572868
  2.0 7.1 %collective-permute-start = (f32[32,16,128]{2,1,0:T(8,128)S(1)}, f32[32,16,128]{2,1,0:T(8,128)S(1)}, u32[]{:S(2)}, u32[]{:S(2)}) collective-permute-start(f32[32,16,128]{2,1,0:T(8,128)S(1)} %get-tuple-element.42), channel_id=1, source_target_pairs={{0,64},{64,128},{128,192},{192,0},{1,65},{65,129},{129,193},{193,1... | collective-permute-start | bytes 786440 | tf_op jit(solution)/shard_map/ppermute | solution.py:702
  4.1 6.6 %collective-permute-start.1 = (f32[32,16,128]{2,1,0:T(8,128)S(1)}, f32[32,16,128]{2,1,0:T(8,128)S(1)}, u32[]{:S(2)}, u32[]{:S(2)}) collective-permute-start(f32[32,16,128]{2,1,0:T(8,128)S(1)} %get-tuple-element.43), channel_id=1, source_target_pairs={{64,0},{128,64},{192,128},{0,192},{65,1},{129,65},{193,129},{1,193... | collective-permute-start | bytes 786440 | tf_op jit(solution)/shard_map/ppermute | solution.py:702
  5.9 8.1 %collective-permute-start.2 = (f32[48,8,128]{2,1,0:T(8,128)S(1)}, f32[48,8,128]{2,1,0:T(8,128)S(1)}, u32[]{:S(2)}, u32[]{:S(2)}) collective-permute-start(f32[48,8,128]{2,1,0:T(8,128)S(1)} %get-tuple-element.46), channel_id=1, source_target_pairs={{0,8},{8,16},{16,24},{24,32},{32,40},{40,48},{48,56},{56,0},{1,9},... | collective-permute-start | bytes 589832 | tf_op jit(solution)/shard_map/ppermute | solution.py:702
  8.5 5.6 %collective-permute-start.3 = (f32[48,8,128]{2,1,0:T(8,128)S(1)}, f32[48,8,128]{2,1,0:T(8,128)S(1)}, u32[]{:S(2)}, u32[]{:S(2)}) collective-permute-start(f32[48,8,128]{2,1,0:T(8,128)S(1)} %get-tuple-element.47), channel_id=1, source_target_pairs={{8,0},{16,8},{24,16},{32,24},{40,32},{48,40},{56,48},{0,56},{9,1},... | collective-permute-start | bytes 589832 | tf_op jit(solution)/shard_map/ppermute | solution.py:702
  10.7 4.8 %collective-permute-start.4 = (f32[20,8,128]{2,1,0:T(8,128)S(1)}, f32[20,8,128]{2,1,0:T(8,128)S(1)}, u32[]{:S(2)}, u32[]{:S(2)}) collective-permute-start(f32[20,8,128]{2,1,0:T(8,128)S(1)} %get-tuple-element.49), channel_id=1, source_target_pairs={{0,8},{8,16},{16,24},{24,32},{32,40},{40,48},{48,56},{56,0},{1,9},... | collective-permute-start | bytes 245768 | tf_op jit(solution)/shard_map/ppermute | solution.py:702
  14.0 3.9 %collective-permute-start.5 = (f32[20,8,128]{2,1,0:T(8,128)S(1)}, f32[20,8,128]{2,1,0:T(8,128)S(1)}, u32[]{:S(2)}, u32[]{:S(2)}) collective-permute-start(f32[20,8,128]{2,1,0:T(8,128)S(1)} %get-tuple-element.50), channel_id=1, source_target_pairs={{8,0},{16,8},{24,16},{32,24},{40,32},{48,40},{56,48},{0,56},{9,1},... | collective-permute-start | bytes 245768 | tf_op jit(solution)/shard_map/ppermute | solution.py:702
  18.1 9.6 %collective-permute-start.8 = (f32[12,8,128]{2,1,0:T(8,128)S(1)}, f32[12,8,128]{2,1,0:T(8,128)S(1)}, u32[]{:S(2)}, u32[]{:S(2)}) collective-permute-start(f32[12,8,128]{2,1,0:T(8,128)S(1)} %get-tuple-element.62), channel_id=1, source_target_pairs={{0,1},{1,2},{2,3},{3,4},{4,5},{5,6},{6,7},{7,0},{8,9},{9,10},{10,1... | collective-permute-start | bytes 147464 | tf_op jit(solution)/shard_map/ppermute | solution.py:702
  19.8 7.9 %collective-permute-start.9 = (f32[12,8,128]{2,1,0:T(8,128)S(1)}, f32[12,8,128]{2,1,0:T(8,128)S(1)}, u32[]{:S(2)}, u32[]{:S(2)}) collective-permute-start(f32[12,8,128]{2,1,0:T(8,128)S(1)} %get-tuple-element.63), channel_id=1, source_target_pairs={{1,0},{2,1},{3,2},{4,3},{5,4},{6,5},{7,6},{0,7},{9,8},{10,9},{11,1... | collective-permute-start | bytes 147464 | tf_op jit(solution)/shard_map/ppermute | solution.py:702
  23.9 3.9 %collective-permute-start.6 = (f32[3,16,128]{2,1,0:T(8,128)S(1)}, f32[3,16,128]{2,1,0:T(8,128)S(1)}, u32[]{:S(2)}, u32[]{:S(2)}) collective-permute-start(f32[3,16,128]{2,1,0:T(8,128)S(1)} %get-tuple-element.60), channel_id=1, source_target_pairs={{0,1},{1,2},{2,3},{3,4},{4,5},{5,6},{6,7},{7,0},{8,9},{9,10},{10,1... | collective-permute-start | bytes 73736 | tf_op jit(solution)/shard_map/ppermute | solution.py:731
  23.9 3.9 %collective-permute-start.7 = (f32[3,16,128]{2,1,0:T(8,128)S(1)}, f32[3,16,128]{2,1,0:T(8,128)S(1)}, u32[]{:S(2)}, u32[]{:S(2)}) collective-permute-start(f32[3,16,128]{2,1,0:T(8,128)S(1)} %get-tuple-element.61), channel_id=1, source_target_pairs={{1,0},{2,1},{3,2},{4,3},{5,4},{6,5},{7,6},{0,7},{9,8},{10,9},{11,1... | collective-permute-start | bytes 73736 | tf_op jit(solution)/shard_map/ppermute | solution.py:732
  27.8 4.0 %copy-start = (f32[8,4,4,16,128]{4,3,2,1,0:T(8,128)S(1)}, f32[8,4,4,16,128]{4,3,2,1,0:T(8,128)}, u32[]{:S(2)}) copy-start(f32[8,4,4,16,128]{4,3,2,1,0:T(8,128)} %q_ref.1) | copy-start | bytes 3145732
  28.9 4.7 %collective-permute-start.10 = (f32[23,8,128]{2,1,0:T(8,128)S(1)}, f32[23,8,128]{2,1,0:T(8,128)S(1)}, u32[]{:S(2)}, u32[]{:S(2)}) collective-permute-start(f32[23,8,128]{2,1,0:T(8,128)S(1)} %get-tuple-element.71), channel_id=1, source_target_pairs={{0,64},{64,128},{128,192},{192,0},{1,65},{65,129},{129,193},{193,1... | collective-permute-start | bytes 282632 | tf_op jit(solution)/shard_map/ppermute | solution.py:702
  30.2 3.4 %collective-permute-start.11 = (f32[23,8,128]{2,1,0:T(8,128)S(1)}, f32[23,8,128]{2,1,0:T(8,128)S(1)}, u32[]{:S(2)}, u32[]{:S(2)}) collective-permute-start(f32[23,8,128]{2,1,0:T(8,128)S(1)} %get-tuple-element.72), channel_id=1, source_target_pairs={{64,0},{128,64},{192,128},{0,192},{65,1},{129,65},{193,129},{1,193... | collective-permute-start | bytes 282632 | tf_op jit(solution)/shard_map/ppermute | solution.py:702
